TPU v7x, 128 devices: a whole 4x4x4 slice. The times are simulated.
128 devices in a mesh: outer: 16 (over z, x_lo, core), inner: 8 (over y, x_hi).
Axes of the slice: x: 4 (x_hi: 2, x_lo: 2; x = x_hi * 2 + x_lo), y: 4, z: 4, core: 2. Of those that a mesh axis runs over, the one named last changes fastest.
Arguments:
- queries: bfloat16 [8, 16384, 128], P(None, ('outer', 'inner')), may hold values from -6 to 6
- key_states: bfloat16 [16384, 128], P(('outer', 'inner')), may hold values from -6 to 6
- value_states: bfloat16 [16384, 128], P(('outer', 'inner')), may hold values from -6 to 6
- outputs: bfloat16 [8, 16384, 128], P(None, ('outer', 'inner')), may hold values from -6 to 6
- grad_outputs: bfloat16 [8, 16384, 128], P(None, ('outer', 'inner')), may hold values from -6 to 6
- log_sums: float32 [8, 16384], P(None, ('outer', 'inner')), may hold values from -1 to 20
- span_order: int32 [256], replicated, may hold values from 0 to 255, as said below
Outputs:
- query_grads: bfloat16 [8, 16384, 128], P(None, ('outer', 'inner'))
- key_grads: bfloat16 [16384, 128], P(('outer', 'inner'))
- value_grads: bfloat16 [16384, 128], P(('outer', 'inner'))
Inputs may be any that keep to these rules, and one draw needn't show every extreme that they name: span_order is a permutation of the 256 position blocks; entries 2 d and 2 d + 1 (the blocks stored on device d) add up to 255.
All inputs are finite; a program needn't handle non-finite values.
Results may differ from a plain program's by a relative error of at most 0.0052.
Values may be sent and summed in bfloat16 or wider, within the bound.
No kernel may reach another device: no remote copies, remote signals or barrier semaphores. Data moves between devices by JAX's collectives and lax.ppermute only.
A program may use at most 64 MiB of HBM per device.

v0:
```python
import functools
import math

import jax
import jax.numpy as jnp
from jax import lax
from jax.experimental import pallas as pl
from jax.experimental.pallas import tpu as pltpu
from jax.sharding import Mesh
from jax.sharding import PartitionSpec as P


f32 = jnp.float32
bf16 = jnp.bfloat16
NT = (((1,), (1,)), ((), ()))
NN = (((1,), (0,)), ((), ()))
LOG2E = 1.0 / math.log(2.0)
AXES = ("zh", "zl", "xl", "c", "yh", "yl", "xh")
KV_AXES = ("zl", "yl", "zh", "yh")
WIDE = 4
UNROLL = 2
LIMIT = 24
STAT_ROWS = 32


def dot(a, b, dims):
    return lax.dot_general(a, b, dims, preferred_element_type=f32)


def kernel(first, last, counts, near, scale, order, sorted_pos, query_block, below, own, *rest):
    if first:
        kv_ref, rest = rest[0], rest[1:]
    else:
        (ks, vs, kt, dk_ref, dv_ref), rest = rest[:5], rest[5:]
    payloads, rest = rest[: len(counts)], rest[len(counts) :]
    near_ref = far_ref = None
    if near:
        near_ref, rest = rest[0], rest[1:]
    if near < sum(counts):
        far_ref, rest = rest[0], rest[1:]
    if first:
        (ks, vs, kt), rest = rest[:3], rest[3:]
    if last:
        dkv_ref, rest = rest[0], rest[1:]
    dk, dv, qd, st, dq = rest
    groups, _, width = qd.shape
    rows = st.shape[2]
    blocks = order.shape[0]
    span = ks.shape[0] // blocks
    chunk = WIDE * span
    if first:
        for r in range(blocks):
            block = kv_ref[order[r]]
            ks[r * span : (r + 1) * span, :] = block[:, :width]
            vs[r * span : (r + 1) * span, :] = block[:, width:]
        for r in range(0, blocks * span, chunk):
            kt[:, r : r + chunk] = ks[r : r + chunk, :].T
        dk[...] = jnp.zeros_like(dk)
        dv[...] = jnp.zeros_like(dv)
    else:
        dk[...] = dk_ref[...]
        dv[...] = dv_ref[...]
    lines = rows // width
    g = 0
    for ref, count in zip(payloads, counts):
        for i in range(count):
            qd[g] = ref[i, : 2 * rows, :]
            terms = ref[i, 2 * rows :, :].astype(f32)
            for kind in range(2):
                t = terms[kind * 3 * lines :]
                t = t[:lines] + t[lines : 2 * lines] + t[2 * lines : 3 * lines]
                st[g, kind : kind + 1, :] = jnp.concatenate(
                    [t[j : j + 1] for j in range(lines)], axis=1
                )
            g += 1

    def unit(g, first, count, size, masked):
        q, do = qd[g, :rows, :], qd[g, rows : 2 * rows, :]
        log_norm, delta = st[g, 0:1, :], st[g, 1:2, :]
        total = None
        for n in range(count):
            at = pl.ds(pl.multiple_of((first + n) * chunk, chunk), size * span)
            k, v = ks[at, :], vs[at, :]
            s = dot(k, q, NT)
            dp = dot(v, do, NT)
            p = jnp.exp2(s * (scale * LOG2E) - log_norm)
            if masked:
                lead = lax.rem(lax.broadcasted_iota(jnp.int32, (span, rows), 1), span)
                lead = lead - lax.broadcasted_iota(jnp.int32, (span, rows), 0)
                seen = [
                    lead + (query_block[g] - sorted_pos[(first + n) * WIDE + j]) * span
                    for j in range(size)
                ]
                p = jnp.where(jnp.concatenate(seen, axis=0) >= 0, p, 0.0)
            ds = (p * (dp - delta)).astype(bf16)
            dv[at, :] += dot(p.astype(bf16), do, NN)
            dk[at, :] += dot(ds, q, NN)
            part = dot(kt[:, at], ds, NN)
            total = part if total is None else total + part
        dq[...] += total

    def group(g, carry):
        dq[...] = jnp.zeros_like(dq)
        whole = below[g] // WIDE
        pairs = whole // UNROLL

        def step(i, carry):
            unit(g, i * UNROLL, UNROLL, WIDE, False)
            return carry

        def single(i, carry):
            unit(g, i, 1, WIDE, False)
            return carry

        lax.fori_loop(0, pairs, step, 0)
        lax.fori_loop(pairs * UNROLL, whole, single, 0)

        rest = below[g] + own[g] - whole * WIDE

        @pl.when((rest > 0) & (rest <= WIDE // 2))
        def _():
            unit(g, whole, 1, WIDE // 2, True)

        @pl.when(rest > WIDE // 2)
        def _():
            unit(g, whole, 1, WIDE, True)

        def store_near():
            for j in range(0, rows, width):
                near_ref[g, j : j + width, :] = dq[:, j : j + width].T

        def store_far():
            for j in range(0, rows, width):
                far_ref[g - near, j : j + width, :] = dq[:, j : j + width].T.astype(bf16)

        if far_ref is None:
            store_near()
        elif near_ref is None:
            store_far()
        else:
            pl.when(g < near)(store_near)
            pl.when(g >= near)(store_far)
        return carry

    lax.fori_loop(0, groups, group, 0)
    if last:
        for r in range(blocks):
            at = pl.ds(r * span, span)
            dkv_ref[order[r]] = jnp.concatenate([dk[at, :], dv[at, :]], axis=1).astype(
                dkv_ref.dtype
            )


def attend(tables, state, payloads, near, first, last):
    counts = tuple(p.shape[0] for p in payloads)
    groups = sum(counts)
    width = payloads[0].shape[2]
    rows = (payloads[0].shape[1] - STAT_ROWS) // 2
    blocks = tables[0].shape[0]
    if first:
        (kv,) = state
        keys = blocks * kv.shape[1]
    else:
        keys = state[0].shape[0]
    span = keys // blocks
    vmem = pl.BlockSpec(memory_space=pltpu.VMEM)
    smem = pl.BlockSpec(memory_space=pltpu.SMEM)
    scale = 1.0 / math.sqrt(width)
    pairs = groups * rows * keys // 2
    totals = [jax.ShapeDtypeStruct((keys, width), f32)] * 2
    out_shape = []
    if near:
        out_shape.append(jax.ShapeDtypeStruct((near, rows, width), f32))
    if near < groups:
        out_shape.append(jax.ShapeDtypeStruct((groups - near, rows, width), bf16))
    scratch = [
        pltpu.VMEM((groups, 2 * rows, width), bf16),
        pltpu.VMEM((groups, 2, rows), f32),
        pltpu.VMEM((width, rows), f32),
    ]
    if first:
        out_shape += [
            jax.ShapeDtypeStruct((keys, width), bf16),
            jax.ShapeDtypeStruct((keys, width), bf16),
            jax.ShapeDtypeStruct((width, keys), bf16),
        ]
    if last:
        out_shape.append(jax.ShapeDtypeStruct((blocks, span, 2 * width), bf16))
        scratch = [pltpu.VMEM((keys, width), f32)] * 2 + scratch
    else:
        out_shape += totals
    out_specs = [vmem] * len(out_shape)
    return pl.pallas_call(
        functools.partial(kernel, first, last, counts, near, scale),
        out_shape=tuple(out_shape),
        in_specs=[smem] * len(tables) + [vmem] * (len(state) + len(payloads)),
        out_specs=tuple(out_specs),
        scratch_shapes=scratch,
        cost_estimate=pl.CostEstimate(
            flops=pairs * width * 20, transcendentals=pairs, bytes_accessed=8 << 20
        ),
        compiler_params=pltpu.CompilerParams(vmem_limit_bytes=LIMIT << 20),
    )(*tables, *state, *payloads)


def copies_kernel(k_ref, v_ref, kv_ref, tile, sems):
    width = k_ref.shape[1]
    count = kv_ref.shape[0]
    reads = [
        pltpu.make_async_copy(ref, tile.at[:, pl.ds(n * width, width)], sems.at[count + n])
        for n, ref in enumerate((k_ref, v_ref))
    ]
    for copy in reads:
        copy.start()
    for copy in reads:
        copy.wait()
    writes = [pltpu.make_async_copy(tile, kv_ref.at[j], sems.at[j]) for j in range(count)]
    for copy in writes:
        copy.start()
    for copy in writes:
        copy.wait()


def copy_out(k, v, count):
    tokens, width = k.shape
    hbm = pltpu.MemorySpace.HBM
    spec = pl.BlockSpec(memory_space=hbm)
    return pl.pallas_call(
        copies_kernel,
        out_shape=jax.ShapeDtypeStruct((count, tokens, 2 * width), k.dtype),
        in_specs=[spec, spec],
        out_specs=spec,
        scratch_shapes=[
            pltpu.VMEM((tokens, 2 * width), k.dtype),
            pltpu.SemaphoreType.DMA((count + 2,)),
        ],
        compiler_params=pltpu.CompilerParams(vmem_limit_bytes=8 << 20),
        name="copies",
    )(*(pltpu.with_memory_space_constraint(a, hbm) for a in (k, v)))


def prepare_kernel(q_ref, do_ref, o_ref, log_ref, mine_ref):
    heads, tokens, width = q_ref.shape
    span = tokens // 2
    rows = heads * span
    ones = jnp.ones((8, width), bf16)
    log_norm = log_ref[...] * LOG2E
    turned = pltpu.roll(log_norm, span, 1)
    lower = lax.broadcasted_iota(jnp.int32, (1, tokens), 1) < span

    def terms(x):
        high = x.astype(bf16)
        rest = x - high.astype(f32)
        middle = rest.astype(bf16)
        low = (rest - middle.astype(f32)).astype(bf16)
        return [high.astype(f32), middle.astype(f32), low.astype(f32)]

    for s in range(2):
        at = slice(s * span, (s + 1) * span)
        mine_ref[s, :rows, :] = q_ref[:, at, :].reshape(rows, width)
        do = do_ref[:, at, :].reshape(rows, width)
        mine_ref[s, rows : 2 * rows, :] = do
        both = do.astype(f32) * o_ref[:, at, :].reshape(rows, width).astype(f32)
        high = both.astype(bf16)
        low = (both - high.astype(f32)).astype(bf16)
        delta = dot(ones, high, NT) + dot(ones, low, NT)
        delta = jnp.concatenate(
            [delta[0:1, j : j + width] for j in range(0, rows, width)], axis=0
        )
        first, second = (log_norm, turned) if s == 0 else (turned, log_norm)
        norms = jnp.concatenate(
            [
                jnp.where(lower, first[j : j + 1], second[j + 1 : j + 2])
                for j in range(0, heads, 2)
            ],
            axis=0,
        )
        pieces = terms(norms) + terms(delta)
        filled = sum(p.shape[0] for p in pieces)
        pieces.append(jnp.zeros((STAT_ROWS - filled, width), f32))
        mine_ref[s, 2 * rows :, :] = jnp.concatenate(pieces, axis=0).astype(bf16)


def local_call(function, out_shape, *args):
    vmem = pl.BlockSpec(memory_space=pltpu.VMEM)
    many = isinstance(out_shape, tuple)
    return pl.pallas_call(
        function,
        out_shape=out_shape,
        in_specs=[vmem] * len(args),
        out_specs=(vmem,) * len(out_shape) if many else vmem,
        compiler_params=pltpu.CompilerParams(vmem_limit_bytes=8 << 20),
    )(*args)


def finish_kernel(scale, parts_ref, dk_ref, dv_ref):
    width = dk_ref.shape[1]
    total = parts_ref[0].astype(f32)
    for j in range(1, parts_ref.shape[0]):
        total = total + parts_ref[j].astype(f32)
    dk_ref[...] = (total[:, :width] * scale).astype(bf16)
    dv_ref[...] = total[:, width:].astype(bf16)


def finish_dq_kernel(scale, own_ref, *rest):
    parts, dq_ref = rest[:-1], rest[-1]
    heads, tokens, width = dq_ref.shape
    span = tokens // 2
    for s in range(2):
        total = own_ref[s]
        for ref in parts:
            total = total + ref[s].astype(f32)
        total = (total * scale).astype(bf16)
        dq_ref[:, s * span : (s + 1) * span, :] = total.reshape(heads, span, width)


def lookup(table, ids):
    hits = ids[:, None] == jnp.arange(table.shape[0], dtype=jnp.int32)[None, :]
    return jnp.sum(jnp.where(hits, table[None, :], 0), axis=1)


def rank(zh, zl, xl, c, yh, yl, xh):
    out = 0
    for bit in (zh, zl, xl, c, yh, yl, xh):
        out = out * 2 + bit
    return out


def x_shift(a, by):
    at = lambda x: (x % 2) * 2 + x // 2
    return lax.ppermute(a, ("xl", "xh"), [(at(x), at((x + by) % 4)) for x in range(4)])


def swap(a):
    return lax.ppermute(a, "c", [(0, 1), (1, 0)])


def spread(a):
    return lax.all_to_all(a, KV_AXES, 0, 0, tiled=True)


def body(q, k, v, o, do, log_sums, span_order):
    heads, tokens, width = q.shape
    span = tokens // 2
    scale = 1.0 / math.sqrt(width)
    zh, zl, xl, c, yh, yl, xh = [lax.axis_index(a) for a in AXES]
    x = xh * 2 + xl

    kv = copy_out(k, v, 16)
    payload = jax.ShapeDtypeStruct((2, heads * tokens + STAT_ROWS, width), bf16)
    mine = local_call(prepare_kernel, payload, q, do, o, log_sums)
    kv = spread(kv).reshape(32, span, 2 * width)
    right = x_shift(mine, 1)
    left = x_shift(mine, -1)
    across = x_shift(mine, 2)

    i16 = jnp.arange(16, dtype=jnp.int32)
    bits = {axis: (i16 >> (3 - n)) & 1 for n, axis in enumerate(KV_AXES)}
    kv_ids = rank(bits["zh"], bits["zl"], xl, c, bits["yh"], bits["yl"], xh)
    q_ids = []
    for near_shifts, far_shifts in (((0,), (0,)), ((3, 1, 2), ()), ((), (3, 1, 2))):
        chosen = [(c, shift) for shift in near_shifts] + [(1 - c, shift) for shift in far_shifts]
        for cc, shift in chosen:
            xx = (x + shift) & 3
            q_ids.append(rank(zh, zl, xx & 1, cc, yh, yl, xx >> 1))
    ids = jnp.concatenate([kv_ids, jnp.stack(q_ids)])
    ids = (ids[:, None] * 2 + jnp.arange(2, dtype=jnp.int32)[None, :]).reshape(48)
    pos = lookup(span_order, ids)
    kv_pos, q_pos = pos[:32], pos[32:]
    place = jnp.sum((kv_pos[None, :] < kv_pos[:, None]).astype(jnp.int32), axis=1)
    hit = place[:, None] == jnp.arange(32, dtype=jnp.int32)[None, :]
    order = jnp.sum(jnp.where(hit, jnp.arange(32, dtype=jnp.int32)[:, None], 0), axis=0)
    sorted_pos = jnp.sum(jnp.where(hit, kv_pos[:, None], 0), axis=0)
    below = jnp.sum((kv_pos[None, :] < q_pos[:, None]).astype(jnp.int32), axis=1)
    own = jnp.sum((kv_pos[None, :] == q_pos[:, None]).astype(jnp.int32), axis=1)

    def tables(start, count):
        at = slice(start, start + count)
        return (order, sorted_pos, q_pos[at], below[at], own[at])

    first = (mine, swap(mine))
    dq, dq_far, *state = attend(tables(0, 4), (kv,), first, 2, True, False)
    near = (right, left, across)
    far = (swap(right), swap(left), swap(across))
    dq_near, dk, dv = attend(tables(4, 6), state, near, 6, False, False)
    state = (*state[:3], dk, dv)
    dq_back, dkv = attend(tables(10, 6), state, far, 0, False, True)
    dq_own = swap(dq_far)
    out = (dq_near + swap(dq_back).astype(f32)).astype(bf16)

    dkv = spread(dkv.reshape(16, tokens, 2 * width))
    shape = jax.ShapeDtypeStruct((tokens, width), bf16)
    dk, dv = local_call(functools.partial(finish_kernel, scale), (shape, shape), dkv)
    parts = [x_shift(out[:2], -1), x_shift(out[2:4], 1), x_shift(out[4:], 2)]
    shape = jax.ShapeDtypeStruct((heads, tokens, width), bf16)
    finish_dq = functools.partial(finish_dq_kernel, scale)
    return local_call(finish_dq, shape, dq, dq_own, *parts), dk, dv


def solution(mesh):
    fine = Mesh(mesh.devices.reshape((2,) * 7), AXES)
    return jax.shard_map(
        body,
        mesh=fine,
        in_specs=(
            P(None, AXES, None),
            P(AXES, None),
            P(AXES, None),
            P(None, AXES, None),
            P(None, AXES, None),
            P(None, AXES),
            P(),
        ),
        out_specs=(P(None, AXES, None), P(AXES, None), P(AXES, None)),
        check_vma=False,
    )
```

profile of v0, /device:TPU:0, one launch (start us, length us, event | category | flops | bytes accessed | tf_op | source)
XLA Modules:
  0.0 100.4 jit_solution(16131485284972595460)
XLA Ops:
  0.6 0.9 copy-done.1
  1.6 0.9 copy-done.2
  2.5 0.9 copy-done.3
  3.5 0.7 copy-done.4
  4.6 1.7 %collective-permute-start.2 = (bf16[2,1056,128]{2,1,0:T(8,128)(2,1)S(1)}, bf16[2,1056,128]{2,1,0:T(8,128)(2,1)}, u32[]{:S(2)}, u32[]{:S(2)}) collective-permute-start(bf16[2,1056,128]{2,1,0:T(8,128)(2,1)S(1)} %shard_map.94.rest_1_), channel_id=1, source_target_pairs={{0,16},{16,1},{1,17},{17,0},{2,18},{18,3},{3,19},{19,2},{4,20},{20... | collective-permute-start | bytes 1622024 | tf_op jit(solution)/shard_map/ppermute | solution.py:331
  6.2 1.6 %collective-permute-start.3 = (bf16[2,1056,128]{2,1,0:T(8,128)(2,1)S(1)}, bf16[2,1056,128]{2,1,0:T(8,128)(2,1)}, u32[]{:S(2)}, u32[]{:S(2)}) collective-permute-start(bf16[2,1056,128]{2,1,0:T(8,128)(2,1)S(1)} %shard_map.94.rest_1_), channel_id=1, source_target_pairs={{0,17},{16,0},{1,16},{17,1},{2,19},{18,2},{3,18},{19,3},{4,21},{20... | collective-permute-start | bytes 1622024 | tf_op jit(solution)/shard_map/ppermute | solution.py:331
  7.9 1.9 %collective-permute-start.4 = (bf16[2,1056,128]{2,1,0:T(8,128)(2,1)S(1)}, bf16[2,1056,128]{2,1,0:T(8,128)(2,1)}, u32[]{:S(2)}, u32[]{:S(2)}) collective-permute-start(bf16[2,1056,128]{2,1,0:T(8,128)(2,1)S(1)} %shard_map.94.rest_1_), channel_id=1, source_target_pairs={{0,1},{16,17},{1,0},{17,16},{2,3},{18,19},{3,2},{19,18},{4,5},{20,... | collective-permute-start | bytes 1622024 | tf_op jit(solution)/shard_map/ppermute | solution.py:331
  9.8 1.9 %copies.1 = bf16[16,128,256]{2,1,0:T(8,128)(2,1)} custom-call(bf16[128,128]{1,0:T(8,128)(2,1)} %k_ref.1, bf16[128,128]{1,0:T(8,128)(2,1)} %v_ref.1), custom_call_target="tpu_custom_call" | custom-call | tf_op jit(solution)/shard_map/copies/pallas_call | solution.py:228
  11.7 8.1 %all-to-all-start = ((bf16[16,128,256]{2,1,0:T(8,128)(2,1)}), bf16[16,128,256]{2,1,0:T(8,128)(2,1)S(1)}, u32[]{:S(2)}, u32[]{:S(2)}) async-start(bf16[16,128,256]{2,1,0:T(8,128)(2,1)} %copies.1), calls=%async_computation | async-start | bytes 2097152 | tf_op jit(solution)/shard_map/all_to_all | solution.py:339
  21.7 11.6 %collective-permute-done.4.rest_7_ = bf16[2,1056,128]{2,1,0:T(8,128)(2,1)} collective-permute-done((bf16[2,1056,128]{2,1,0:T(8,128)(2,1)S(1)}, bf16[2,1056,128]{2,1,0:T(8,128)(2,1)}, u32[]{:S(2)}, u32[]{:S(2)}) %collective-permute-start.4) | collective-permute-done | bytes 540704 | tf_op jit(solution)/shard_map/ppermute | solution.py:331
  33.2 2.7 %all-to-all-done = bf16[16,128,256]{2,1,0:T(8,128)(2,1)S(1)} async-done(((bf16[16,128,256]{2,1,0:T(8,128)(2,1)}), bf16[16,128,256]{2,1,0:T(8,128)(2,1)S(1)}, u32[]{:S(2)}, u32[]{:S(2)}) %all-to-all-start) | async-done | bytes 1048608 | tf_op jit(solution)/shard_map/all_to_all | solution.py:339
  35.9 9.0 %shard_map.95 = (f32[2,512,128]{2,1,0:T(8,128)S(1)}, bf16[2,512,128]{2,1,0:T(8,128)(2,1)S(1)}, bf16[2048,128]{1,0:T(8,128)(2,1)S(1)}, bf16[2048,128]{1,0:T(8,128...) custom-call(s32[32]{0:T(128)S(1)} %get-tuple-element.34.order, ...), custom_call_target="tpu_custom_call" | custom-call | flops 5368709120 | bytes 8388608 | tf_op jit(solution)/shard_map/pallas_call | solution.py:193
  44.9 0.7 copy-done.5
  45.6 13.1 %shard_map.96 = (f32[6,512,128]{2,1,0:T(8,128)S(1)}, f32[2048,128]{1,0:T(8,128)S(1)}, f32[2048,128]{1,0:T(8,128)S(1)}) custom-call(s32[32]{0:T(128)S(1)} %get-tuple-element.34.order, s32[32]{0:T(128)S(1)} %get-tuple-element.33.sorted_pos, s32[6]{0:T(128)S(1)} %get-tuple-element.43.query_block, s32[6]{0:T(128)S(1)} %get-tuple-element.44.below, ...), custom_call_target="tpu_custom_call" | custom-call | flops 8053063680 | bytes 8388608 | tf_op jit(solution)/shard_map/pallas_call | solution.py:193
  58.7 14.4 %shard_map.97 = (bf16[6,512,128]{2,1,0:T(8,128)(2,1)}, bf16[32,64,256]{2,1,0:T(8,128)(2,1)S(1)}) custom-call(s32[32]{0:T(128)S(1)} %get-tuple-element.34.order, s32[32]{0:T(128)S(1)} %get-tuple-element.33.sorted_pos, s32[6]{0:T(128)S(1)} %get-tuple-element.42.query_block, s32[6]{0:T(128)S(1)} %get-tuple-element.45.below, s32[6]{0:T(128)S(1)} %get-tuple-element.38.own, ...), custom_call_target="tpu_custom_call" | custom-call | flops 8053063680 | bytes 8388608 | tf_op jit(solution)/shard_map/pallas_call | solution.py:193
  73.1 1.0 copy-done
  74.1 5.9 %all-to-all-start.1 = ((bf16[16,128,256]{2,1,0:T(8,128)(2,1)}), bf16[16,128,256]{2,1,0:T(8,128)(2,1)S(1)}, u32[]{:S(2)}, u32[]{:S(2)}) async-start(bf16[16,128,256]{2,1,0:T(8,128)(2,1)} %bitcast.14), calls=%async_computation.1 | async-start | bytes 2097152 | tf_op jit(solution)/shard_map/all_to_all | solution.py:339
  80.3 1.3 %add_convert_fusion = bf16[6,512,128]{2,1,0:T(8,128)(2,1)S(1)} fusion(f32[6,512,128]{2,1,0:T(8,128)S(1)} %get-tuple-element.24, bf16[6,512,128]{2,1,0:T(8,128)(2,1)} %collective-permute-done.8), kind=kLoop, calls=%fused_computation | loop fusion | flops 1179648 | bytes 3145728 | tf_op jit(solution)/shard_map/convert_element_type | solution.py:389
  81.6 2.8 %collective-permute-start.9 = (bf16[2,512,128]{2,1,0:T(8,128)(2,1)S(1)}, bf16[2,512,128]{2,1,0:T(8,128)(2,1)S(1)}, u32[]{:S(2)}, u32[]{:S(2)}) collective-permute-start(bf16[2,512,128]{2,1,0:T(8,128)(2,1)S(1)} %get-tuple-element.37), channel_id=1, source_target_pairs={{0,17},{16,0},{1,16},{17,1},{2,19},{18,2},{3,18},{19,3},{4,21},{20... | collective-permute-start | bytes 786440 | tf_op jit(solution)/shard_map/ppermute | solution.py:331
  84.4 1.5 %collective-permute-start.11 = (bf16[2,512,128]{2,1,0:T(8,128)(2,1)S(1)}, bf16[2,512,128]{2,1,0:T(8,128)(2,1)S(1)}, u32[]{:S(2)}, u32[]{:S(2)}) collective-permute-start(bf16[2,512,128]{2,1,0:T(8,128)(2,1)S(1)} %get-tuple-element.35), channel_id=1, source_target_pairs={{0,1},{16,17},{1,0},{17,16},{2,3},{18,19},{3,2},{19,18},{4,5},{20,... | collective-permute-start | bytes 786440 | tf_op jit(solution)/shard_map/ppermute | solution.py:331
  86.0 10.8 %all-to-all-done.1.parts_ref = bf16[16,128,256]{2,1,0:T(8,128)(2,1)S(1)} async-done(((bf16[16,128,256]{2,1,0:T(8,128)(2,1)}), bf16[16,128,256]{2,1,0:T(8,128)(2,1)S(1)}, u32[]{:S(2)}, u32[]{:S(2)}) %all-to-all-start.1) | async-done | bytes 1048608 | tf_op jit(solution)/shard_map/all_to_all | solution.py:339
  96.8 0.8 shard_map.99
  97.6 1.9 %collective-permute-done.10.rest_2_ = bf16[2,512,128]{2,1,0:T(8,128)(2,1)S(1)} collective-permute-done((bf16[2,512,128]{2,1,0:T(8,128)(2,1)S(1)}, bf16[2,512,128]{2,1,0:T(8,128)(2,1)S(1)}, u32[]{:S(2)}, u32[]{:S(2)}) %collective-permute-start.10) | collective-permute-done | bytes 262176 | tf_op jit(solution)/shard_map/ppermute | solution.py:331
  99.5 0.9 shard_map.98
  (40 shorter events, 2.5 us)
Async XLA Ops:
  0.6 1.0 copy-start.1
  1.6 0.9 copy-start.2
  2.5 0.9 copy-start.3
  3.5 0.7 copy-start.4
  4.5 15.7 %copy-start.6 = (s32[256]{0:T(256)S(1)}, s32[256]{0:T(256)}, u32[]{:S(2)}) copy-start(s32[256]{0:T(256)} %param.13) | copy-start | bytes 3076
  4.5 28.8 %collective-permute-start = (bf16[2,1056,128]{2,1,0:T(8,128)(2,1)S(1)}, bf16[2,1056,128]{2,1,0:T(8,128)(2,1)S(1)}, u32[]{:S(2)}, u32[]{:S(2)}) collective-permute-start(bf16[2,1056,128]{2,1,0:T(8,128)(2,1)S(1)} %shard_map.94.rest_1_), channel_id=1, source_target_pairs={{0,8},{8,0},{1,9},{9,1},{2,10},{10,2},{3,11},{11,3},{4,12},{12,4},... | collective-permute-start | bytes 1622024 | tf_op jit(solution)/shard_map/ppermute | solution.py:335
  4.6 16.5 %collective-permute-start.2 = (bf16[2,1056,128]{2,1,0:T(8,128)(2,1)S(1)}, bf16[2,1056,128]{2,1,0:T(8,128)(2,1)}, u32[]{:S(2)}, u32[]{:S(2)}) collective-permute-start(bf16[2,1056,128]{2,1,0:T(8,128)(2,1)S(1)} %shard_map.94.rest_1_), channel_id=1, source_target_pairs={{0,16},{16,1},{1,17},{17,0},{2,18},{18,3},{3,19},{19,2},{4,20},{20... | collective-permute-start | bytes 1622024 | tf_op jit(solution)/shard_map/ppermute | solution.py:331
  6.2 15.3 %collective-permute-start.3 = (bf16[2,1056,128]{2,1,0:T(8,128)(2,1)S(1)}, bf16[2,1056,128]{2,1,0:T(8,128)(2,1)}, u32[]{:S(2)}, u32[]{:S(2)}) collective-permute-start(bf16[2,1056,128]{2,1,0:T(8,128)(2,1)S(1)} %shard_map.94.rest_1_), channel_id=1, source_target_pairs={{0,17},{16,0},{1,16},{17,1},{2,19},{18,2},{3,18},{19,3},{4,21},{20... | collective-permute-start | bytes 1622024 | tf_op jit(solution)/shard_map/ppermute | solution.py:331
  7.9 25.4 %collective-permute-start.4 = (bf16[2,1056,128]{2,1,0:T(8,128)(2,1)S(1)}, bf16[2,1056,128]{2,1,0:T(8,128)(2,1)}, u32[]{:S(2)}, u32[]{:S(2)}) collective-permute-start(bf16[2,1056,128]{2,1,0:T(8,128)(2,1)S(1)} %shard_map.94.rest_1_), channel_id=1, source_target_pairs={{0,1},{16,17},{1,0},{17,16},{2,3},{18,19},{3,2},{19,18},{4,5},{20,... | collective-permute-start | bytes 1622024 | tf_op jit(solution)/shard_map/ppermute | solution.py:331
  11.7 24.2 %all-to-all-start = ((bf16[16,128,256]{2,1,0:T(8,128)(2,1)}), bf16[16,128,256]{2,1,0:T(8,128)(2,1)S(1)}, u32[]{:S(2)}, u32[]{:S(2)}) async-start(bf16[16,128,256]{2,1,0:T(8,128)(2,1)} %copies.1), calls=%async_computation | async-start | bytes 2097152 | tf_op jit(solution)/shard_map/all_to_all | solution.py:339
  21.1 37.6 %collective-permute-start.5 = (bf16[2,1056,128]{2,1,0:T(8,128)(2,1)}, bf16[2,1056,128]{2,1,0:T(8,128)(2,1)}, u32[]{:S(2)}, u32[]{:S(2)}) collective-permute-start(bf16[2,1056,128]{2,1,0:T(8,128)(2,1)} %collective-permute-done.2.rest_5_), channel_id=1, source_target_pairs={{0,8},{8,0},{1,9},{9,1},{2,10},{10,2},{3,11},{11,3},{4,12},{12,4},... | collective-permute-start | bytes 1622024 | tf_op jit(solution)/shard_map/ppermute | solution.py:335
  21.5 37.2 %collective-permute-start.6 = (bf16[2,1056,128]{2,1,0:T(8,128)(2,1)}, bf16[2,1056,128]{2,1,0:T(8,128)(2,1)}, u32[]{:S(2)}, u32[]{:S(2)}) collective-permute-start(bf16[2,1056,128]{2,1,0:T(8,128)(2,1)} %collective-permute-done.3.rest_6_), channel_id=1, source_target_pairs={{0,8},{8,0},{1,9},{9,1},{2,10},{10,2},{3,11},{11,3},{4,12},{12,4},... | collective-permute-start | bytes 1622024 | tf_op jit(solution)/shard_map/ppermute | solution.py:335
  33.2 25.5 %collective-permute-start.7 = (bf16[2,1056,128]{2,1,0:T(8,128)(2,1)}, bf16[2,1056,128]{2,1,0:T(8,128)(2,1)}, u32[]{:S(2)}, u32[]{:S(2)}) collective-permute-start(bf16[2,1056,128]{2,1,0:T(8,128)(2,1)} %collective-permute-done.4.rest_7_), channel_id=1, source_target_pairs={{0,8},{8,0},{1,9},{9,1},{2,10},{10,2},{3,11},{11,3},{4,12},{12,4},... | collective-permute-start | bytes 1622024 | tf_op jit(solution)/shard_map/ppermute | solution.py:335
  44.9 0.7 copy-start.5
  73.1 1.0 copy-start
  74.1 6.2 %collective-permute-start.8 = (bf16[6,512,128]{2,1,0:T(8,128)(2,1)}, bf16[6,512,128]{2,1,0:T(8,128)(2,1)}, u32[]{:S(2)}, u32[]{:S(2)}) collective-permute-start(bf16[6,512,128]{2,1,0:T(8,128)(2,1)} %get-tuple-element.27), channel_id=1, source_target_pairs={{0,8},{8,0},{1,9},{9,1},{2,10},{10,2},{3,11},{11,3},{4,12},{12,4},... | collective-permute-start | bytes 2359304 | tf_op jit(solution)/shard_map/ppermute | solution.py:335
  74.1 22.7 %all-to-all-start.1 = ((bf16[16,128,256]{2,1,0:T(8,128)(2,1)}), bf16[16,128,256]{2,1,0:T(8,128)(2,1)S(1)}, u32[]{:S(2)}, u32[]{:S(2)}) async-start(bf16[16,128,256]{2,1,0:T(8,128)(2,1)} %bitcast.14), calls=%async_computation.1 | async-start | bytes 2097152 | tf_op jit(solution)/shard_map/all_to_all | solution.py:339
  80.0 17.6 %collective-permute-start.1 = (bf16[2,512,128]{2,1,0:T(8,128)(2,1)}, bf16[2,512,128]{2,1,0:T(8,128)(2,1)S(1)}, u32[]{:S(2)}, u32[]{:S(2)}) collective-permute-start(bf16[2,512,128]{2,1,0:T(8,128)(2,1)} %copy-done.5), channel_id=1, source_target_pairs={{0,8},{8,0},{1,9},{9,1},{2,10},{10,2},{3,11},{11,3},{4,12},{12,4},... | collective-permute-start | bytes 786440 | tf_op jit(solution)/shard_map/ppermute | solution.py:335
  81.6 15.9 %collective-permute-start.9 = (bf16[2,512,128]{2,1,0:T(8,128)(2,1)S(1)}, bf16[2,512,128]{2,1,0:T(8,128)(2,1)S(1)}, u32[]{:S(2)}, u32[]{:S(2)}) collective-permute-start(bf16[2,512,128]{2,1,0:T(8,128)(2,1)S(1)} %get-tuple-element.37), channel_id=1, source_target_pairs={{0,17},{16,0},{1,16},{17,1},{2,19},{18,2},{3,18},{19,3},{4,21},{20... | collective-permute-start | bytes 786440 | tf_op jit(solution)/shard_map/ppermute | solution.py:331
  84.4 15.0 %collective-permute-start.10 = (bf16[2,512,128]{2,1,0:T(8,128)(2,1)S(1)}, bf16[2,512,128]{2,1,0:T(8,128)(2,1)S(1)}, u32[]{:S(2)}, u32[]{:S(2)}) collective-permute-start(bf16[2,512,128]{2,1,0:T(8,128)(2,1)S(1)} %get-tuple-element.36), channel_id=1, source_target_pairs={{0,16},{16,1},{1,17},{17,0},{2,18},{18,3},{3,19},{19,2},{4,20},{20... | collective-permute-start | bytes 786440 | tf_op jit(solution)/shard_map/ppermute | solution.py:331
  84.4 15.0 %collective-permute-start.11 = (bf16[2,512,128]{2,1,0:T(8,128)(2,1)S(1)}, bf16[2,512,128]{2,1,0:T(8,128)(2,1)S(1)}, u32[]{:S(2)}, u32[]{:S(2)}) collective-permute-start(bf16[2,512,128]{2,1,0:T(8,128)(2,1)S(1)} %get-tuple-element.35), channel_id=1, source_target_pairs={{0,1},{16,17},{1,0},{17,16},{2,3},{18,19},{3,2},{19,18},{4,5},{20,... | collective-permute-start | bytes 786440 | tf_op jit(solution)/shard_map/ppermute | solution.py:331
where the time goes:
time: 101 us; the launch traced here: 100 us
  Pallas kernels  40.2 us (40%)
  waiting for transfers between devices  27.4 us (27%)
  starting transfers between devices  24.1 us (24%)
  local copies, waits for them, and re-layouts  5.74 us (6%)
  other arithmetic  2.02 us (2%)
    pallas_call x3, Pallas kernels, attend(): pl.pallas_call(functools.partial(kernel, first, last, counts, near, scale...  36.4 us
    all_to_all x2, starting transfers between devices, spread(): return lax.all_to_all(a, KV_AXES, 0, 0, tiled=True)  13.9 us
    ppermute x6, waiting for transfers between devices, x_shift(): lax.ppermute(a, ('xl', 'xh'), [(at(x), at((x + by) % 4)) for x in range(4)])  13.9 us
    all_to_all x2, waiting for transfers between devices, spread(): return lax.all_to_all(a, KV_AXES, 0, 0, tiled=True)  13.5 us
    ppermute x6, starting transfers between devices, x_shift(): lax.ppermute(a, ('xl', 'xh'), [(at(x), at((x + by) % 4)) for x in range(4)])  9.59 us
    unnamed x14, local copies, waits for them, and re-layouts  5.21 us
  transfers between devices with their start and end apart: 14, of which 5 were waited for; matrix products, arithmetic and copies ran while one was open for 3% of the time, Pallas kernels for 25%

commit v1 on v0

--- a/solution.py
+++ b/solution.py
@@ -203,46 +203,13 @@
     )(*tables, *state, *payloads)
 
 
-def copies_kernel(k_ref, v_ref, kv_ref, tile, sems):
-    width = k_ref.shape[1]
-    count = kv_ref.shape[0]
-    reads = [
-        pltpu.make_async_copy(ref, tile.at[:, pl.ds(n * width, width)], sems.at[count + n])
-        for n, ref in enumerate((k_ref, v_ref))
-    ]
-    for copy in reads:
-        copy.start()
-    for copy in reads:
-        copy.wait()
-    writes = [pltpu.make_async_copy(tile, kv_ref.at[j], sems.at[j]) for j in range(count)]
-    for copy in writes:
-        copy.start()
-    for copy in writes:
-        copy.wait()
-
-
-def copy_out(k, v, count):
-    tokens, width = k.shape
-    hbm = pltpu.MemorySpace.HBM
-    spec = pl.BlockSpec(memory_space=hbm)
-    return pl.pallas_call(
-        copies_kernel,
-        out_shape=jax.ShapeDtypeStruct((count, tokens, 2 * width), k.dtype),
-        in_specs=[spec, spec],
-        out_specs=spec,
-        scratch_shapes=[
-            pltpu.VMEM((tokens, 2 * width), k.dtype),
-            pltpu.SemaphoreType.DMA((count + 2,)),
-        ],
-        compiler_params=pltpu.CompilerParams(vmem_limit_bytes=8 << 20),
-        name="copies",
-    )(*(pltpu.with_memory_space_constraint(a, hbm) for a in (k, v)))
-
-
-def prepare_kernel(q_ref, do_ref, o_ref, log_ref, mine_ref):
+def prepare_kernel(q_ref, do_ref, o_ref, log_ref, k_ref, v_ref, mine_ref, kv_ref):
     heads, tokens, width = q_ref.shape
     span = tokens // 2
     rows = heads * span
+    for j in range(kv_ref.shape[0]):
+        kv_ref[j, :, :width] = k_ref[...]
+        kv_ref[j, :, width:] = v_ref[...]
     ones = jnp.ones((8, width), bf16)
     log_norm = log_ref[...] * LOG2E
     turned = pltpu.roll(log_norm, span, 1)
@@ -281,7 +248,7 @@
         mine_ref[s, 2 * rows :, :] = jnp.concatenate(pieces, axis=0).astype(bf16)
 
 
-def local_call(function, out_shape, *args):
+def local_call(function, out_shape, *args, limit=8):
     vmem = pl.BlockSpec(memory_space=pltpu.VMEM)
     many = isinstance(out_shape, tuple)
     return pl.pallas_call(
@@ -289,7 +256,7 @@
         out_shape=out_shape,
         in_specs=[vmem] * len(args),
         out_specs=(vmem,) * len(out_shape) if many else vmem,
-        compiler_params=pltpu.CompilerParams(vmem_limit_bytes=8 << 20),
+        compiler_params=pltpu.CompilerParams(vmem_limit_bytes=limit << 20),
     )(*args)
 
 
@@ -346,9 +313,11 @@
     zh, zl, xl, c, yh, yl, xh = [lax.axis_index(a) for a in AXES]
     x = xh * 2 + xl
 
-    kv = copy_out(k, v, 16)
     payload = jax.ShapeDtypeStruct((2, heads * tokens + STAT_ROWS, width), bf16)
-    mine = local_call(prepare_kernel, payload, q, do, o, log_sums)
+    copies = jax.ShapeDtypeStruct((16, tokens, 2 * width), bf16)
+    mine, kv = local_call(
+        prepare_kernel, (payload, copies), q, do, o, log_sums, k, v, limit=60
+    )
     kv = spread(kv).reshape(32, span, 2 * width)
     right = x_shift(mine, 1)
     left = x_shift(mine, -1)

time: 101 us -> 99.8 us (0.988)
  local copies, waits for them, and re-layouts: 5.74 us -> 2.21 us
  starting transfers between devices: 24.1 us -> 26 us
    unnamed x14 -> x8, local copies, waits for them, and re-layouts: 5.21 us -> 1.68 us
    ppermute x6, waiting for transfers between devices: 13.9 us -> 16.2 us  [x_shift(): lax.ppermute(a, ('xl', 'xh'), [(at(x), at((x + by) % 4)) for x in range(4)])]
    pallas_call x3, Pallas kernels: 1.91 us -> 4.21 us  [local_call(): pl.pallas_call(function, out_shape=out_shape, in_specs=[vmem] * len(args)...]
    all_to_all x2, waiting for transfers between devices: 13.5 us -> 11.4 us  [spread(): return lax.all_to_all(a, KV_AXES, 0, 0, tiled=True)]
    all_to_all x2, starting transfers between devices: 13.9 us -> 16.1 us  [spread(): return lax.all_to_all(a, KV_AXES, 0, 0, tiled=True)]
    pallas_call x1 -> x0, Pallas kernels: 1.91 us -> none  [copy_out(): pl.pallas_call(copies_kernel, out_shape=jax.ShapeDtypeStruct((count, toke...]
  transfers between devices with their start and end apart: 14 -> 14, of which waited for: 5 -> 6; matrix products, arithmetic and copies ran while one was open for 3% -> 3% of each run, Pallas kernels for 25% -> 23%
where the time goes in v1:
time: 99.8 us; the launch traced here: 99.2 us
  Pallas kernels  40.6 us (41%)
  waiting for transfers between devices  27.6 us (28%)
  starting transfers between devices  26 us (26%)
  local copies, waits for them, and re-layouts  2.21 us (2%)
  other arithmetic  2.02 us (2%)
    pallas_call x3, Pallas kernels, attend(): pl.pallas_call(functools.partial(kernel, first, last, counts, near, scale...  36.4 us
    ppermute x6, waiting for transfers between devices, x_shift(): lax.ppermute(a, ('xl', 'xh'), [(at(x), at((x + by) % 4)) for x in range(4)])  16.2 us
    all_to_all x2, starting transfers between devices, spread(): return lax.all_to_all(a, KV_AXES, 0, 0, tiled=True)  16.1 us
    all_to_all x2, waiting for transfers between devices, spread(): return lax.all_to_all(a, KV_AXES, 0, 0, tiled=True)  11.4 us
    ppermute x6, starting transfers between devices, x_shift(): lax.ppermute(a, ('xl', 'xh'), [(at(x), at((x + by) % 4)) for x in range(4)])  9.59 us
    pallas_call x3, Pallas kernels, local_call(): pl.pallas_call(function, out_shape=out_shape, in_specs=[vmem] * len(args)...  4.21 us
  transfers between devices with their start and end apart: 14, of which 6 were waited for; matrix products, arithmetic and copies ran while one was open for 3% of the time, Pallas kernels for 23%

profile of v1, /device:TPU:0, one launch (start us, length us, event | category | flops | bytes accessed | tf_op | source)
XLA Modules:
  0.0 99.2 jit_solution(9499409817945724525)
XLA Ops:
  0.6 2.6 %shard_map.94 = (bf16[2,1056,128]{2,1,0:T(8,128)(2,1)}, bf16[16,128,256]{2,1,0:T(8,128)(2,1)}) custom-call(bf16[8,128,128]{2,1,0:T(8,128)(2,1)} %q_ref.1, bf16[8,128,128]{2,1,0:T(8,128)(2,1)} %do_ref.1, bf16[8,128,128]{2,1,0:T(8,128)(2,1)} %o_ref.1, f32[8,128]{1,0:T(8,128)} %log_ref.1, bf16[128,128]{1,0:T(8,128)(2,1)} %k_ref.1, bf16[128,128]{1,0:T(8,128)(2,1)} %v_ref.1), custom_call_target="tpu_custom_call" | custom-call | tf_op jit(solution)/shard_map/pallas_call | solution.py:254
  3.2 1.7 %collective-permute-start.2 = (bf16[2,1056,128]{2,1,0:T(8,128)(2,1)}, bf16[2,1056,128]{2,1,0:T(8,128)(2,1)}, u32[]{:S(2)}, u32[]{:S(2)}) collective-permute-start(bf16[2,1056,128]{2,1,0:T(8,128)(2,1)} %get-tuple-element.20.rest_1_), channel_id=1, source_target_pairs={{0,16},{16,1},{1,17},{17,0},{2,18},{18,3},{3,19},{19,2},{4,20},{20... | collective-permute-start | bytes 1622024 | tf_op jit(solution)/shard_map/ppermute | solution.py:298
  4.9 1.6 %collective-permute-start.3 = (bf16[2,1056,128]{2,1,0:T(8,128)(2,1)}, bf16[2,1056,128]{2,1,0:T(8,128)(2,1)}, u32[]{:S(2)}, u32[]{:S(2)}) collective-permute-start(bf16[2,1056,128]{2,1,0:T(8,128)(2,1)} %get-tuple-element.20.rest_1_), channel_id=1, source_target_pairs={{0,17},{16,0},{1,16},{17,1},{2,19},{18,2},{3,18},{19,3},{4,21},{20... | collective-permute-start | bytes 1622024 | tf_op jit(solution)/shard_map/ppermute | solution.py:298
  6.5 1.9 %collective-permute-start.4 = (bf16[2,1056,128]{2,1,0:T(8,128)(2,1)}, bf16[2,1056,128]{2,1,0:T(8,128)(2,1)}, u32[]{:S(2)}, u32[]{:S(2)}) collective-permute-start(bf16[2,1056,128]{2,1,0:T(8,128)(2,1)} %get-tuple-element.20.rest_1_), channel_id=1, source_target_pairs={{0,1},{16,17},{1,0},{17,16},{2,3},{18,19},{3,2},{19,18},{4,5},{20,... | collective-permute-start | bytes 1622024 | tf_op jit(solution)/shard_map/ppermute | solution.py:298
  8.5 8.0 %all-to-all-start = ((bf16[16,128,256]{2,1,0:T(8,128)(2,1)}), bf16[16,128,256]{2,1,0:T(8,128)(2,1)S(1)}, u32[]{:S(2)}, u32[]{:S(2)}) async-start(bf16[16,128,256]{2,1,0:T(8,128)(2,1)} %get-tuple-element.19), calls=%async_computation | async-start | bytes 2097152 | tf_op jit(solution)/shard_map/all_to_all | solution.py:306
  17.5 0.2 convert_reduce_fusion.1
  17.8 1.6 %collective-permute-done.2.rest_5_ = bf16[2,1056,128]{2,1,0:T(8,128)(2,1)} collective-permute-done((bf16[2,1056,128]{2,1,0:T(8,128)(2,1)}, bf16[2,1056,128]{2,1,0:T(8,128)(2,1)}, u32[]{:S(2)}, u32[]{:S(2)}) %collective-permute-start.2) | collective-permute-done | bytes 540704 | tf_op jit(solution)/shard_map/ppermute | solution.py:298
  19.5 0.9 collective-permute-done.3.rest_6_
  20.4 11.8 %collective-permute-done.4.rest_7_ = bf16[2,1056,128]{2,1,0:T(8,128)(2,1)} collective-permute-done((bf16[2,1056,128]{2,1,0:T(8,128)(2,1)}, bf16[2,1056,128]{2,1,0:T(8,128)(2,1)}, u32[]{:S(2)}, u32[]{:S(2)}) %collective-permute-start.4) | collective-permute-done | bytes 540704 | tf_op jit(solution)/shard_map/ppermute | solution.py:298
  32.1 0.6 all-to-all-done
  32.7 9.0 %shard_map.95 = (f32[2,512,128]{2,1,0:T(8,128)S(1)}, bf16[2,512,128]{2,1,0:T(8,128)(2,1)S(1)}, bf16[2048,128]{1,0:T(8,128)(2,1)S(1)}, bf16[2048,128]{1,0:T(8,128...) custom-call(s32[32]{0:T(128)S(1)} %get-tuple-element.38.order, ...), custom_call_target="tpu_custom_call" | custom-call | flops 5368709120 | bytes 8388608 | tf_op jit(solution)/shard_map/pallas_call | solution.py:193
  41.7 0.7 copy-done.2
  42.4 13.1 %shard_map.96 = (f32[6,512,128]{2,1,0:T(8,128)S(1)}, f32[2048,128]{1,0:T(8,128)S(1)}, f32[2048,128]{1,0:T(8,128)S(1)}) custom-call(s32[32]{0:T(128)S(1)} %get-tuple-element.38.order, s32[32]{0:T(128)S(1)} %get-tuple-element.37.sorted_pos, s32[6]{0:T(128)S(1)} %get-tuple-element.47.query_block, s32[6]{0:T(128)S(1)} %get-tuple-element.48.below, ...), custom_call_target="tpu_custom_call" | custom-call | flops 8053063680 | bytes 8388608 | tf_op jit(solution)/shard_map/pallas_call | solution.py:193
  55.5 14.4 %shard_map.97 = (bf16[6,512,128]{2,1,0:T(8,128)(2,1)}, bf16[32,64,256]{2,1,0:T(8,128)(2,1)S(1)}) custom-call(s32[32]{0:T(128)S(1)} %get-tuple-element.38.order, s32[32]{0:T(128)S(1)} %get-tuple-element.37.sorted_pos, s32[6]{0:T(128)S(1)} %get-tuple-element.46.query_block, s32[6]{0:T(128)S(1)} %get-tuple-element.49.below, s32[6]{0:T(128)S(1)} %get-tuple-element.42.own, ...), custom_call_target="tpu_custom_call" | custom-call | flops 8053063680 | bytes 8388608 | tf_op jit(solution)/shard_map/pallas_call | solution.py:193
  69.8 1.0 copy-done
  70.8 8.0 %all-to-all-start.1 = ((bf16[16,128,256]{2,1,0:T(8,128)(2,1)}), bf16[16,128,256]{2,1,0:T(8,128)(2,1)S(1)}, u32[]{:S(2)}, u32[]{:S(2)}) async-start(bf16[16,128,256]{2,1,0:T(8,128)(2,1)} %bitcast.14), calls=%async_computation.1 | async-start | bytes 2097152 | tf_op jit(solution)/shard_map/all_to_all | solution.py:306
  78.8 0.3 collective-permute-start.1
  79.1 1.3 %add_convert_fusion = bf16[6,512,128]{2,1,0:T(8,128)(2,1)S(1)} fusion(f32[6,512,128]{2,1,0:T(8,128)S(1)} %get-tuple-element.28, bf16[6,512,128]{2,1,0:T(8,128)(2,1)} %collective-permute-done.8), kind=kLoop, calls=%fused_computation | loop fusion | flops 1179648 | bytes 3145728 | tf_op jit(solution)/shard_map/convert_element_type | solution.py:358
  80.5 2.8 %collective-permute-start.9 = (bf16[2,512,128]{2,1,0:T(8,128)(2,1)S(1)}, bf16[2,512,128]{2,1,0:T(8,128)(2,1)S(1)}, u32[]{:S(2)}, u32[]{:S(2)}) collective-permute-start(bf16[2,512,128]{2,1,0:T(8,128)(2,1)S(1)} %get-tuple-element.41), channel_id=1, source_target_pairs={{0,17},{16,0},{1,16},{17,1},{2,19},{18,2},{3,18},{19,3},{4,21},{20... | collective-permute-start | bytes 786440 | tf_op jit(solution)/shard_map/ppermute | solution.py:298
  83.3 1.5 %collective-permute-start.11 = (bf16[2,512,128]{2,1,0:T(8,128)(2,1)S(1)}, bf16[2,512,128]{2,1,0:T(8,128)(2,1)S(1)}, u32[]{:S(2)}, u32[]{:S(2)}) collective-permute-start(bf16[2,512,128]{2,1,0:T(8,128)(2,1)S(1)} %get-tuple-element.39), channel_id=1, source_target_pairs={{0,1},{16,17},{1,0},{17,16},{2,3},{18,19},{3,2},{19,18},{4,5},{20,... | collective-permute-start | bytes 786440 | tf_op jit(solution)/shard_map/ppermute | solution.py:298
  84.9 10.8 %all-to-all-done.1.parts_ref = bf16[16,128,256]{2,1,0:T(8,128)(2,1)S(1)} async-done(((bf16[16,128,256]{2,1,0:T(8,128)(2,1)}), bf16[16,128,256]{2,1,0:T(8,128)(2,1)S(1)}, u32[]{:S(2)}, u32[]{:S(2)}) %all-to-all-start.1) | async-done | bytes 1048608 | tf_op jit(solution)/shard_map/all_to_all | solution.py:306
  95.7 0.8 shard_map.99
  96.4 1.9 %collective-permute-done.10.rest_2_ = bf16[2,512,128]{2,1,0:T(8,128)(2,1)S(1)} collective-permute-done((bf16[2,512,128]{2,1,0:T(8,128)(2,1)S(1)}, bf16[2,512,128]{2,1,0:T(8,128)(2,1)S(1)}, u32[]{:S(2)}, u32[]{:S(2)}) %collective-permute-start.10) | collective-permute-done | bytes 262176 | tf_op jit(solution)/shard_map/ppermute | solution.py:298
  98.4 0.9 shard_map.98
  (33 shorter events, 1.1 us)
Async XLA Ops:
  0.6 16.3 %copy-start.3 = (s32[256]{0:T(256)S(1)}, s32[256]{0:T(256)}, u32[]{:S(2)}) copy-start(s32[256]{0:T(256)} %param.13) | copy-start | bytes 3076
  3.2 29.5 %copy-start.1 = (bf16[2,1056,128]{2,1,0:T(8,128)(2,1)S(1)}, bf16[2,1056,128]{2,1,0:T(8,128)(2,1)}, u32[]{:S(2)}) copy-start(bf16[2,1056,128]{2,1,0:T(8,128)(2,1)} %get-tuple-element.20.rest_1_) | copy-start | bytes 1622020
  3.2 28.9 %collective-permute-start = (bf16[2,1056,128]{2,1,0:T(8,128)(2,1)}, bf16[2,1056,128]{2,1,0:T(8,128)(2,1)S(1)}, u32[]{:S(2)}, u32[]{:S(2)}) collective-permute-start(bf16[2,1056,128]{2,1,0:T(8,128)(2,1)} %get-tuple-element.20.rest_1_), channel_id=1, source_target_pairs={{0,8},{8,0},{1,9},{9,1},{2,10},{10,2},{3,11},{11,3},{4,12},{12,4},... | collective-permute-start | bytes 1622024 | tf_op jit(solution)/shard_map/ppermute | solution.py:302
  3.2 16.2 %collective-permute-start.2 = (bf16[2,1056,128]{2,1,0:T(8,128)(2,1)}, bf16[2,1056,128]{2,1,0:T(8,128)(2,1)}, u32[]{:S(2)}, u32[]{:S(2)}) collective-permute-start(bf16[2,1056,128]{2,1,0:T(8,128)(2,1)} %get-tuple-element.20.rest_1_), channel_id=1, source_target_pairs={{0,16},{16,1},{1,17},{17,0},{2,18},{18,3},{3,19},{19,2},{4,20},{20... | collective-permute-start | bytes 1622024 | tf_op jit(solution)/shard_map/ppermute | solution.py:298
  4.9 15.5 %collective-permute-start.3 = (bf16[2,1056,128]{2,1,0:T(8,128)(2,1)}, bf16[2,1056,128]{2,1,0:T(8,128)(2,1)}, u32[]{:S(2)}, u32[]{:S(2)}) collective-permute-start(bf16[2,1056,128]{2,1,0:T(8,128)(2,1)} %get-tuple-element.20.rest_1_), channel_id=1, source_target_pairs={{0,17},{16,0},{1,16},{17,1},{2,19},{18,2},{3,18},{19,3},{4,21},{20... | collective-permute-start | bytes 1622024 | tf_op jit(solution)/shard_map/ppermute | solution.py:298
  6.5 25.6 %collective-permute-start.4 = (bf16[2,1056,128]{2,1,0:T(8,128)(2,1)}, bf16[2,1056,128]{2,1,0:T(8,128)(2,1)}, u32[]{:S(2)}, u32[]{:S(2)}) collective-permute-start(bf16[2,1056,128]{2,1,0:T(8,128)(2,1)} %get-tuple-element.20.rest_1_), channel_id=1, source_target_pairs={{0,1},{16,17},{1,0},{17,16},{2,3},{18,19},{3,2},{19,18},{4,5},{20,... | collective-permute-start | bytes 1622024 | tf_op jit(solution)/shard_map/ppermute | solution.py:298
  8.5 24.2 %all-to-all-start = ((bf16[16,128,256]{2,1,0:T(8,128)(2,1)}), bf16[16,128,256]{2,1,0:T(8,128)(2,1)S(1)}, u32[]{:S(2)}, u32[]{:S(2)}) async-start(bf16[16,128,256]{2,1,0:T(8,128)(2,1)} %get-tuple-element.19), calls=%async_computation | async-start | bytes 2097152 | tf_op jit(solution)/shard_map/all_to_all | solution.py:306
  19.4 36.0 %collective-permute-start.5 = (bf16[2,1056,128]{2,1,0:T(8,128)(2,1)}, bf16[2,1056,128]{2,1,0:T(8,128)(2,1)}, u32[]{:S(2)}, u32[]{:S(2)}) collective-permute-start(bf16[2,1056,128]{2,1,0:T(8,128)(2,1)} %collective-permute-done.2.rest_5_), channel_id=1, source_target_pairs={{0,8},{8,0},{1,9},{9,1},{2,10},{10,2},{3,11},{11,3},{4,12},{12,4},... | collective-permute-start | bytes 1622024 | tf_op jit(solution)/shard_map/ppermute | solution.py:302
  20.4 35.1 %collective-permute-start.6 = (bf16[2,1056,128]{2,1,0:T(8,128)(2,1)}, bf16[2,1056,128]{2,1,0:T(8,128)(2,1)}, u32[]{:S(2)}, u32[]{:S(2)}) collective-permute-start(bf16[2,1056,128]{2,1,0:T(8,128)(2,1)} %collective-permute-done.3.rest_6_), channel_id=1, source_target_pairs={{0,8},{8,0},{1,9},{9,1},{2,10},{10,2},{3,11},{11,3},{4,12},{12,4},... | collective-permute-start | bytes 1622024 | tf_op jit(solution)/shard_map/ppermute | solution.py:302
  32.1 23.3 %collective-permute-start.7 = (bf16[2,1056,128]{2,1,0:T(8,128)(2,1)}, bf16[2,1056,128]{2,1,0:T(8,128)(2,1)}, u32[]{:S(2)}, u32[]{:S(2)}) collective-permute-start(bf16[2,1056,128]{2,1,0:T(8,128)(2,1)} %collective-permute-done.4.rest_7_), channel_id=1, source_target_pairs={{0,8},{8,0},{1,9},{9,1},{2,10},{10,2},{3,11},{11,3},{4,12},{12,4},... | collective-permute-start | bytes 1622024 | tf_op jit(solution)/shard_map/ppermute | solution.py:302
  41.7 0.7 copy-start.2
  69.8 1.0 copy-start
  70.8 8.3 %collective-permute-start.8 = (bf16[6,512,128]{2,1,0:T(8,128)(2,1)}, bf16[6,512,128]{2,1,0:T(8,128)(2,1)}, u32[]{:S(2)}, u32[]{:S(2)}) collective-permute-start(bf16[6,512,128]{2,1,0:T(8,128)(2,1)} %get-tuple-element.31), channel_id=1, source_target_pairs={{0,8},{8,0},{1,9},{9,1},{2,10},{10,2},{3,11},{11,3},{4,12},{12,4},... | collective-permute-start | bytes 2359304 | tf_op jit(solution)/shard_map/ppermute | solution.py:302
  70.8 24.9 %all-to-all-start.1 = ((bf16[16,128,256]{2,1,0:T(8,128)(2,1)}), bf16[16,128,256]{2,1,0:T(8,128)(2,1)S(1)}, u32[]{:S(2)}, u32[]{:S(2)}) async-start(bf16[16,128,256]{2,1,0:T(8,128)(2,1)} %bitcast.14), calls=%async_computation.1 | async-start | bytes 2097152 | tf_op jit(solution)/shard_map/all_to_all | solution.py:306
  78.8 17.6 %collective-permute-start.1 = (bf16[2,512,128]{2,1,0:T(8,128)(2,1)}, bf16[2,512,128]{2,1,0:T(8,128)(2,1)S(1)}, u32[]{:S(2)}, u32[]{:S(2)}) collective-permute-start(bf16[2,512,128]{2,1,0:T(8,128)(2,1)} %copy-done.2), channel_id=1, source_target_pairs={{0,8},{8,0},{1,9},{9,1},{2,10},{10,2},{3,11},{11,3},{4,12},{12,4},... | collective-permute-start | bytes 786440 | tf_op jit(solution)/shard_map/ppermute | solution.py:302
  80.5 15.9 %collective-permute-start.9 = (bf16[2,512,128]{2,1,0:T(8,128)(2,1)S(1)}, bf16[2,512,128]{2,1,0:T(8,128)(2,1)S(1)}, u32[]{:S(2)}, u32[]{:S(2)}) collective-permute-start(bf16[2,512,128]{2,1,0:T(8,128)(2,1)S(1)} %get-tuple-element.41), channel_id=1, source_target_pairs={{0,17},{16,0},{1,16},{17,1},{2,19},{18,2},{3,18},{19,3},{4,21},{20... | collective-permute-start | bytes 786440 | tf_op jit(solution)/shard_map/ppermute | solution.py:298
  83.3 15.0 %collective-permute-start.10 = (bf16[2,512,128]{2,1,0:T(8,128)(2,1)S(1)}, bf16[2,512,128]{2,1,0:T(8,128)(2,1)S(1)}, u32[]{:S(2)}, u32[]{:S(2)}) collective-permute-start(bf16[2,512,128]{2,1,0:T(8,128)(2,1)S(1)} %get-tuple-element.40), channel_id=1, source_target_pairs={{0,16},{16,1},{1,17},{17,0},{2,18},{18,3},{3,19},{19,2},{4,20},{20... | collective-permute-start | bytes 786440 | tf_op jit(solution)/shard_map/ppermute | solution.py:298
  83.3 15.0 %collective-permute-start.11 = (bf16[2,512,128]{2,1,0:T(8,128)(2,1)S(1)}, bf16[2,512,128]{2,1,0:T(8,128)(2,1)S(1)}, u32[]{:S(2)}, u32[]{:S(2)}) collective-permute-start(bf16[2,512,128]{2,1,0:T(8,128)(2,1)S(1)} %get-tuple-element.39), channel_id=1, source_target_pairs={{0,1},{16,17},{1,0},{17,16},{2,3},{18,19},{3,2},{19,18},{4,5},{20,... | collective-permute-start | bytes 786440 | tf_op jit(solution)/shard_map/ppermute | solution.py:298

commit v2 on v1

--- a/solution.py
+++ b/solution.py
@@ -18,7 +18,7 @@
 AXES = ("zh", "zl", "xl", "c", "yh", "yl", "xh")
 KV_AXES = ("zl", "yl", "zh", "yh")
 WIDE = 4
-UNROLL = 2
+UNROLLS = (4, 2, 1)
 LIMIT = 24
 STAT_ROWS = 32
 
@@ -102,19 +102,17 @@
     def group(g, carry):
         dq[...] = jnp.zeros_like(dq)
         whole = below[g] // WIDE
-        pairs = whole // UNROLL
-
-        def step(i, carry):
-            unit(g, i * UNROLL, UNROLL, WIDE, False)
-            return carry
-
-        def single(i, carry):
-            unit(g, i, 1, WIDE, False)
-            return carry
-
-        lax.fori_loop(0, pairs, step, 0)
-        lax.fori_loop(pairs * UNROLL, whole, single, 0)
-
+        done = 0
+        for count in UNROLLS:
+            start = done
+            turns = (whole - start) // count
+
+            def step(i, carry, start=start, count=count):
+                unit(g, start + i * count, count, WIDE, False)
+                return carry
+
+            lax.fori_loop(0, turns, step, 0)
+            done = start + turns * count
         rest = below[g] + own[g] - whole * WIDE
 
         @pl.when((rest > 0) & (rest <= WIDE // 2))

time: 99.8 us -> 98.7 us (0.989)
  Pallas kernels: 40.6 us -> 39.3 us
    pallas_call x3, Pallas kernels: 36.4 us -> 35.1 us  [attend(): pl.pallas_call(functools.partial(kernel, first, last, counts, near, scale...]
  transfers between devices with their start and end apart: 14 -> 14, of which waited for: 6 -> 6; matrix products, arithmetic and copies ran while one was open for 3% -> 3% of each run, Pallas kernels for 23% -> 22%
where the time goes in v2:
time: 98.7 us; the launch traced here: 98.1 us
  Pallas kernels  39.3 us (40%)
  waiting for transfers between devices  27.6 us (28%)
  starting transfers between devices  26.1 us (26%)
  local copies, waits for them, and re-layouts  2.21 us (2%)
  other arithmetic  2.02 us (2%)
    pallas_call x3, Pallas kernels, attend(): pl.pallas_call(functools.partial(kernel, first, last, counts, near, scale...  35.1 us
    all_to_all x2, starting transfers between devices, spread(): return lax.all_to_all(a, KV_AXES, 0, 0, tiled=True)  16.2 us
    ppermute x6, waiting for transfers between devices, x_shift(): lax.ppermute(a, ('xl', 'xh'), [(at(x), at((x + by) % 4)) for x in range(4)])  16.2 us
    all_to_all x2, waiting for transfers between devices, spread(): return lax.all_to_all(a, KV_AXES, 0, 0, tiled=True)  11.4 us
    ppermute x6, starting transfers between devices, x_shift(): lax.ppermute(a, ('xl', 'xh'), [(at(x), at((x + by) % 4)) for x in range(4)])  9.57 us
    pallas_call x3, Pallas kernels, local_call(): pl.pallas_call(function, out_shape=out_shape, in_specs=[vmem] * len(args)...  4.21 us
  transfers between devices with their start and end apart: 14, of which 6 were waited for; matrix products, arithmetic and copies ran while one was open for 3% of the time, Pallas kernels for 22%

profile of v2, /device:TPU:0, one launch (start us, length us, event | category | flops | bytes accessed | tf_op | source)
XLA Modules:
  0.0 98.1 jit_solution(17190478217498056566)
XLA Ops:
  0.6 2.6 %shard_map.94 = (bf16[2,1056,128]{2,1,0:T(8,128)(2,1)}, bf16[16,128,256]{2,1,0:T(8,128)(2,1)}) custom-call(bf16[8,128,128]{2,1,0:T(8,128)(2,1)} %q_ref.1, bf16[8,128,128]{2,1,0:T(8,128)(2,1)} %do_ref.1, bf16[8,128,128]{2,1,0:T(8,128)(2,1)} %o_ref.1, f32[8,128]{1,0:T(8,128)} %log_ref.1, bf16[128,128]{1,0:T(8,128)(2,1)} %k_ref.1, bf16[128,128]{1,0:T(8,128)(2,1)} %v_ref.1), custom_call_target="tpu_custom_call" | custom-call | tf_op jit(solution)/shard_map/pallas_call | solution.py:252
  3.2 1.7 %collective-permute-start.2 = (bf16[2,1056,128]{2,1,0:T(8,128)(2,1)}, bf16[2,1056,128]{2,1,0:T(8,128)(2,1)}, u32[]{:S(2)}, u32[]{:S(2)}) collective-permute-start(bf16[2,1056,128]{2,1,0:T(8,128)(2,1)} %get-tuple-element.20.rest_1_), channel_id=1, source_target_pairs={{0,16},{16,1},{1,17},{17,0},{2,18},{18,3},{3,19},{19,2},{4,20},{20... | collective-permute-start | bytes 1622024 | tf_op jit(solution)/shard_map/ppermute | solution.py:296
  4.9 1.6 %collective-permute-start.3 = (bf16[2,1056,128]{2,1,0:T(8,128)(2,1)}, bf16[2,1056,128]{2,1,0:T(8,128)(2,1)}, u32[]{:S(2)}, u32[]{:S(2)}) collective-permute-start(bf16[2,1056,128]{2,1,0:T(8,128)(2,1)} %get-tuple-element.20.rest_1_), channel_id=1, source_target_pairs={{0,17},{16,0},{1,16},{17,1},{2,19},{18,2},{3,18},{19,3},{4,21},{20... | collective-permute-start | bytes 1622024 | tf_op jit(solution)/shard_map/ppermute | solution.py:296
  6.5 1.9 %collective-permute-start.4 = (bf16[2,1056,128]{2,1,0:T(8,128)(2,1)}, bf16[2,1056,128]{2,1,0:T(8,128)(2,1)}, u32[]{:S(2)}, u32[]{:S(2)}) collective-permute-start(bf16[2,1056,128]{2,1,0:T(8,128)(2,1)} %get-tuple-element.20.rest_1_), channel_id=1, source_target_pairs={{0,1},{16,17},{1,0},{17,16},{2,3},{18,19},{3,2},{19,18},{4,5},{20,... | collective-permute-start | bytes 1622024 | tf_op jit(solution)/shard_map/ppermute | solution.py:296
  8.5 8.0 %all-to-all-start = ((bf16[16,128,256]{2,1,0:T(8,128)(2,1)}), bf16[16,128,256]{2,1,0:T(8,128)(2,1)S(1)}, u32[]{:S(2)}, u32[]{:S(2)}) async-start(bf16[16,128,256]{2,1,0:T(8,128)(2,1)} %get-tuple-element.19), calls=%async_computation | async-start | bytes 2097152 | tf_op jit(solution)/shard_map/all_to_all | solution.py:304
  17.5 0.2 convert_reduce_fusion.1
  17.8 1.6 %collective-permute-done.2.rest_5_ = bf16[2,1056,128]{2,1,0:T(8,128)(2,1)} collective-permute-done((bf16[2,1056,128]{2,1,0:T(8,128)(2,1)}, bf16[2,1056,128]{2,1,0:T(8,128)(2,1)}, u32[]{:S(2)}, u32[]{:S(2)}) %collective-permute-start.2) | collective-permute-done | bytes 540704 | tf_op jit(solution)/shard_map/ppermute | solution.py:296
  19.5 0.9 collective-permute-done.3.rest_6_
  20.4 11.8 %collective-permute-done.4.rest_7_ = bf16[2,1056,128]{2,1,0:T(8,128)(2,1)} collective-permute-done((bf16[2,1056,128]{2,1,0:T(8,128)(2,1)}, bf16[2,1056,128]{2,1,0:T(8,128)(2,1)}, u32[]{:S(2)}, u32[]{:S(2)}) %collective-permute-start.4) | collective-permute-done | bytes 540704 | tf_op jit(solution)/shard_map/ppermute | solution.py:296
  32.1 0.6 all-to-all-done
  32.7 8.7 %shard_map.95 = (f32[2,512,128]{2,1,0:T(8,128)S(1)}, bf16[2,512,128]{2,1,0:T(8,128)(2,1)S(1)}, bf16[2048,128]{1,0:T(8,128)(2,1)S(1)}, bf16[2048,128]{1,0:T(8,128...) custom-call(s32[32]{0:T(128)S(1)} %get-tuple-element.38.order, ...), custom_call_target="tpu_custom_call" | custom-call | flops 5368709120 | bytes 8388608 | tf_op jit(solution)/shard_map/pallas_call | solution.py:191
  41.4 0.7 copy-done.2
  42.1 12.5 %shard_map.96 = (f32[6,512,128]{2,1,0:T(8,128)S(1)}, f32[2048,128]{1,0:T(8,128)S(1)}, f32[2048,128]{1,0:T(8,128)S(1)}) custom-call(s32[32]{0:T(128)S(1)} %get-tuple-element.38.order, s32[32]{0:T(128)S(1)} %get-tuple-element.37.sorted_pos, s32[6]{0:T(128)S(1)} %get-tuple-element.47.query_block, s32[6]{0:T(128)S(1)} %get-tuple-element.48.below, ...), custom_call_target="tpu_custom_call" | custom-call | flops 8053063680 | bytes 8388608 | tf_op jit(solution)/shard_map/pallas_call | solution.py:191
  54.6 13.9 %shard_map.97 = (bf16[6,512,128]{2,1,0:T(8,128)(2,1)}, bf16[32,64,256]{2,1,0:T(8,128)(2,1)S(1)}) custom-call(s32[32]{0:T(128)S(1)} %get-tuple-element.38.order, s32[32]{0:T(128)S(1)} %get-tuple-element.37.sorted_pos, s32[6]{0:T(128)S(1)} %get-tuple-element.46.query_block, s32[6]{0:T(128)S(1)} %get-tuple-element.49.below, s32[6]{0:T(128)S(1)} %get-tuple-element.42.own, ...), custom_call_target="tpu_custom_call" | custom-call | flops 8053063680 | bytes 8388608 | tf_op jit(solution)/shard_map/pallas_call | solution.py:191
  68.6 1.0 copy-done
  69.5 8.2 %all-to-all-start.1 = ((bf16[16,128,256]{2,1,0:T(8,128)(2,1)}), bf16[16,128,256]{2,1,0:T(8,128)(2,1)S(1)}, u32[]{:S(2)}, u32[]{:S(2)}) async-start(bf16[16,128,256]{2,1,0:T(8,128)(2,1)} %bitcast.14), calls=%async_computation.1 | async-start | bytes 2097152 | tf_op jit(solution)/shard_map/all_to_all | solution.py:304
  77.7 0.3 collective-permute-start.1
  78.0 1.3 %add_convert_fusion = bf16[6,512,128]{2,1,0:T(8,128)(2,1)S(1)} fusion(f32[6,512,128]{2,1,0:T(8,128)S(1)} %get-tuple-element.28, bf16[6,512,128]{2,1,0:T(8,128)(2,1)} %collective-permute-done.8), kind=kLoop, calls=%fused_computation | loop fusion | flops 1179648 | bytes 3145728 | tf_op jit(solution)/shard_map/convert_element_type | solution.py:356
  79.4 2.8 %collective-permute-start.9 = (bf16[2,512,128]{2,1,0:T(8,128)(2,1)S(1)}, bf16[2,512,128]{2,1,0:T(8,128)(2,1)S(1)}, u32[]{:S(2)}, u32[]{:S(2)}) collective-permute-start(bf16[2,512,128]{2,1,0:T(8,128)(2,1)S(1)} %get-tuple-element.41), channel_id=1, source_target_pairs={{0,17},{16,0},{1,16},{17,1},{2,19},{18,2},{3,18},{19,3},{4,21},{20... | collective-permute-start | bytes 786440 | tf_op jit(solution)/shard_map/ppermute | solution.py:296
  82.2 1.5 %collective-permute-start.11 = (bf16[2,512,128]{2,1,0:T(8,128)(2,1)S(1)}, bf16[2,512,128]{2,1,0:T(8,128)(2,1)S(1)}, u32[]{:S(2)}, u32[]{:S(2)}) collective-permute-start(bf16[2,512,128]{2,1,0:T(8,128)(2,1)S(1)} %get-tuple-element.39), channel_id=1, source_target_pairs={{0,1},{16,17},{1,0},{17,16},{2,3},{18,19},{3,2},{19,18},{4,5},{20,... | collective-permute-start | bytes 786440 | tf_op jit(solution)/shard_map/ppermute | solution.py:296
  83.7 10.8 %all-to-all-done.1.parts_ref = bf16[16,128,256]{2,1,0:T(8,128)(2,1)S(1)} async-done(((bf16[16,128,256]{2,1,0:T(8,128)(2,1)}), bf16[16,128,256]{2,1,0:T(8,128)(2,1)S(1)}, u32[]{:S(2)}, u32[]{:S(2)}) %all-to-all-start.1) | async-done | bytes 1048608 | tf_op jit(solution)/shard_map/all_to_all | solution.py:304
  94.6 0.8 shard_map.99
  95.3 1.9 %collective-permute-done.10.rest_2_ = bf16[2,512,128]{2,1,0:T(8,128)(2,1)S(1)} collective-permute-done((bf16[2,512,128]{2,1,0:T(8,128)(2,1)S(1)}, bf16[2,512,128]{2,1,0:T(8,128)(2,1)S(1)}, u32[]{:S(2)}, u32[]{:S(2)}) %collective-permute-start.10) | collective-permute-done | bytes 262176 | tf_op jit(solution)/shard_map/ppermute | solution.py:296
  97.2 0.9 shard_map.98
  (33 shorter events, 1.1 us)
Async XLA Ops:
  0.6 16.3 %copy-start.3 = (s32[256]{0:T(256)S(1)}, s32[256]{0:T(256)}, u32[]{:S(2)}) copy-start(s32[256]{0:T(256)} %param.13) | copy-start | bytes 3076
  3.2 29.5 %copy-start.1 = (bf16[2,1056,128]{2,1,0:T(8,128)(2,1)S(1)}, bf16[2,1056,128]{2,1,0:T(8,128)(2,1)}, u32[]{:S(2)}) copy-start(bf16[2,1056,128]{2,1,0:T(8,128)(2,1)} %get-tuple-element.20.rest_1_) | copy-start | bytes 1622020
  3.2 28.9 %collective-permute-start = (bf16[2,1056,128]{2,1,0:T(8,128)(2,1)}, bf16[2,1056,128]{2,1,0:T(8,128)(2,1)S(1)}, u32[]{:S(2)}, u32[]{:S(2)}) collective-permute-start(bf16[2,1056,128]{2,1,0:T(8,128)(2,1)} %get-tuple-element.20.rest_1_), channel_id=1, source_target_pairs={{0,8},{8,0},{1,9},{9,1},{2,10},{10,2},{3,11},{11,3},{4,12},{12,4},... | collective-permute-start | bytes 1622024 | tf_op jit(solution)/shard_map/ppermute | solution.py:300
  3.2 16.2 %collective-permute-start.2 = (bf16[2,1056,128]{2,1,0:T(8,128)(2,1)}, bf16[2,1056,128]{2,1,0:T(8,128)(2,1)}, u32[]{:S(2)}, u32[]{:S(2)}) collective-permute-start(bf16[2,1056,128]{2,1,0:T(8,128)(2,1)} %get-tuple-element.20.rest_1_), channel_id=1, source_target_pairs={{0,16},{16,1},{1,17},{17,0},{2,18},{18,3},{3,19},{19,2},{4,20},{20... | collective-permute-start | bytes 1622024 | tf_op jit(solution)/shard_map/ppermute | solution.py:296
  4.9 15.5 %collective-permute-start.3 = (bf16[2,1056,128]{2,1,0:T(8,128)(2,1)}, bf16[2,1056,128]{2,1,0:T(8,128)(2,1)}, u32[]{:S(2)}, u32[]{:S(2)}) collective-permute-start(bf16[2,1056,128]{2,1,0:T(8,128)(2,1)} %get-tuple-element.20.rest_1_), channel_id=1, source_target_pairs={{0,17},{16,0},{1,16},{17,1},{2,19},{18,2},{3,18},{19,3},{4,21},{20... | collective-permute-start | bytes 1622024 | tf_op jit(solution)/shard_map/ppermute | solution.py:296
  6.5 25.6 %collective-permute-start.4 = (bf16[2,1056,128]{2,1,0:T(8,128)(2,1)}, bf16[2,1056,128]{2,1,0:T(8,128)(2,1)}, u32[]{:S(2)}, u32[]{:S(2)}) collective-permute-start(bf16[2,1056,128]{2,1,0:T(8,128)(2,1)} %get-tuple-element.20.rest_1_), channel_id=1, source_target_pairs={{0,1},{16,17},{1,0},{17,16},{2,3},{18,19},{3,2},{19,18},{4,5},{20,... | collective-permute-start | bytes 1622024 | tf_op jit(solution)/shard_map/ppermute | solution.py:296
  8.5 24.2 %all-to-all-start = ((bf16[16,128,256]{2,1,0:T(8,128)(2,1)}), bf16[16,128,256]{2,1,0:T(8,128)(2,1)S(1)}, u32[]{:S(2)}, u32[]{:S(2)}) async-start(bf16[16,128,256]{2,1,0:T(8,128)(2,1)} %get-tuple-element.19), calls=%async_computation | async-start | bytes 2097152 | tf_op jit(solution)/shard_map/all_to_all | solution.py:304
  19.4 35.1 %collective-permute-start.5 = (bf16[2,1056,128]{2,1,0:T(8,128)(2,1)}, bf16[2,1056,128]{2,1,0:T(8,128)(2,1)}, u32[]{:S(2)}, u32[]{:S(2)}) collective-permute-start(bf16[2,1056,128]{2,1,0:T(8,128)(2,1)} %collective-permute-done.2.rest_5_), channel_id=1, source_target_pairs={{0,8},{8,0},{1,9},{9,1},{2,10},{10,2},{3,11},{11,3},{4,12},{12,4},... | collective-permute-start | bytes 1622024 | tf_op jit(solution)/shard_map/ppermute | solution.py:300
  20.4 34.2 %collective-permute-start.6 = (bf16[2,1056,128]{2,1,0:T(8,128)(2,1)}, bf16[2,1056,128]{2,1,0:T(8,128)(2,1)}, u32[]{:S(2)}, u32[]{:S(2)}) collective-permute-start(bf16[2,1056,128]{2,1,0:T(8,128)(2,1)} %collective-permute-done.3.rest_6_), channel_id=1, source_target_pairs={{0,8},{8,0},{1,9},{9,1},{2,10},{10,2},{3,11},{11,3},{4,12},{12,4},... | collective-permute-start | bytes 1622024 | tf_op jit(solution)/shard_map/ppermute | solution.py:300
  32.1 22.5 %collective-permute-start.7 = (bf16[2,1056,128]{2,1,0:T(8,128)(2,1)}, bf16[2,1056,128]{2,1,0:T(8,128)(2,1)}, u32[]{:S(2)}, u32[]{:S(2)}) collective-permute-start(bf16[2,1056,128]{2,1,0:T(8,128)(2,1)} %collective-permute-done.4.rest_7_), channel_id=1, source_target_pairs={{0,8},{8,0},{1,9},{9,1},{2,10},{10,2},{3,11},{11,3},{4,12},{12,4},... | collective-permute-start | bytes 1622024 | tf_op jit(solution)/shard_map/ppermute | solution.py:300
  41.4 0.7 copy-start.2
  68.6 1.0 copy-start
  69.5 8.5 %collective-permute-start.8 = (bf16[6,512,128]{2,1,0:T(8,128)(2,1)}, bf16[6,512,128]{2,1,0:T(8,128)(2,1)}, u32[]{:S(2)}, u32[]{:S(2)}) collective-permute-start(bf16[6,512,128]{2,1,0:T(8,128)(2,1)} %get-tuple-element.31), channel_id=1, source_target_pairs={{0,8},{8,0},{1,9},{9,1},{2,10},{10,2},{3,11},{11,3},{4,12},{12,4},... | collective-permute-start | bytes 2359304 | tf_op jit(solution)/shard_map/ppermute | solution.py:300
  69.5 25.0 %all-to-all-start.1 = ((bf16[16,128,256]{2,1,0:T(8,128)(2,1)}), bf16[16,128,256]{2,1,0:T(8,128)(2,1)S(1)}, u32[]{:S(2)}, u32[]{:S(2)}) async-start(bf16[16,128,256]{2,1,0:T(8,128)(2,1)} %bitcast.14), calls=%async_computation.1 | async-start | bytes 2097152 | tf_op jit(solution)/shard_map/all_to_all | solution.py:304
  77.7 17.6 %collective-permute-start.1 = (bf16[2,512,128]{2,1,0:T(8,128)(2,1)}, bf16[2,512,128]{2,1,0:T(8,128)(2,1)S(1)}, u32[]{:S(2)}, u32[]{:S(2)}) collective-permute-start(bf16[2,512,128]{2,1,0:T(8,128)(2,1)} %copy-done.2), channel_id=1, source_target_pairs={{0,8},{8,0},{1,9},{9,1},{2,10},{10,2},{3,11},{11,3},{4,12},{12,4},... | collective-permute-start | bytes 786440 | tf_op jit(solution)/shard_map/ppermute | solution.py:300
  79.4 15.9 %collective-permute-start.9 = (bf16[2,512,128]{2,1,0:T(8,128)(2,1)S(1)}, bf16[2,512,128]{2,1,0:T(8,128)(2,1)S(1)}, u32[]{:S(2)}, u32[]{:S(2)}) collective-permute-start(bf16[2,512,128]{2,1,0:T(8,128)(2,1)S(1)} %get-tuple-element.41), channel_id=1, source_target_pairs={{0,17},{16,0},{1,16},{17,1},{2,19},{18,2},{3,18},{19,3},{4,21},{20... | collective-permute-start | bytes 786440 | tf_op jit(solution)/shard_map/ppermute | solution.py:296
  82.2 15.0 %collective-permute-start.10 = (bf16[2,512,128]{2,1,0:T(8,128)(2,1)S(1)}, bf16[2,512,128]{2,1,0:T(8,128)(2,1)S(1)}, u32[]{:S(2)}, u32[]{:S(2)}) collective-permute-start(bf16[2,512,128]{2,1,0:T(8,128)(2,1)S(1)} %get-tuple-element.40), channel_id=1, source_target_pairs={{0,16},{16,1},{1,17},{17,0},{2,18},{18,3},{3,19},{19,2},{4,20},{20... | collective-permute-start | bytes 786440 | tf_op jit(solution)/shard_map/ppermute | solution.py:296
  82.2 15.0 %collective-permute-start.11 = (bf16[2,512,128]{2,1,0:T(8,128)(2,1)S(1)}, bf16[2,512,128]{2,1,0:T(8,128)(2,1)S(1)}, u32[]{:S(2)}, u32[]{:S(2)}) collective-permute-start(bf16[2,512,128]{2,1,0:T(8,128)(2,1)S(1)} %get-tuple-element.39), channel_id=1, source_target_pairs={{0,1},{16,17},{1,0},{17,16},{2,3},{18,19},{3,2},{19,18},{4,5},{20,... | collective-permute-start | bytes 786440 | tf_op jit(solution)/shard_map/ppermute | solution.py:296

commit v3 on v2

--- a/solution.py
+++ b/solution.py
@@ -18,7 +18,7 @@
 AXES = ("zh", "zl", "xl", "c", "yh", "yl", "xh")
 KV_AXES = ("zl", "yl", "zh", "yh")
 WIDE = 4
-UNROLLS = (4, 2, 1)
+UNROLLS = (4, 3, 2, 1)
 LIMIT = 24
 STAT_ROWS = 32
 
@@ -115,13 +115,11 @@
             done = start + turns * count
         rest = below[g] + own[g] - whole * WIDE
 
-        @pl.when((rest > 0) & (rest <= WIDE // 2))
-        def _():
-            unit(g, whole, 1, WIDE // 2, True)
-
-        @pl.when(rest > WIDE // 2)
-        def _():
-            unit(g, whole, 1, WIDE, True)
+        for size in range(1, WIDE + 1):
+
+            @pl.when(rest == size)
+            def _(size=size):
+                unit(g, whole, 1, size, True)
 
         def store_near():
             for j in range(0, rows, width):

time: 98.7 us -> 98.2 us (level)
  no operation moved by 1% of the time
where the time goes in v3:
time: 98.2 us; the launch traced here: 97.7 us
  Pallas kernels  39.1 us (40%)
  waiting for transfers between devices  27.6 us (28%)
  starting transfers between devices  25.9 us (26%)
  local copies, waits for them, and re-layouts  2.21 us (2%)
  other arithmetic  2.02 us (2%)
    pallas_call x3, Pallas kernels, attend(): pl.pallas_call(functools.partial(kernel, first, last, counts, near, scale...  34.9 us
    ppermute x6, waiting for transfers between devices, x_shift(): lax.ppermute(a, ('xl', 'xh'), [(at(x), at((x + by) % 4)) for x in range(4)])  16.5 us
    all_to_all x2, starting transfers between devices, spread(): return lax.all_to_all(a, KV_AXES, 0, 0, tiled=True)  15.7 us
    all_to_all x2, waiting for transfers between devices, spread(): return lax.all_to_all(a, KV_AXES, 0, 0, tiled=True)  11.1 us
    ppermute x6, starting transfers between devices, x_shift(): lax.ppermute(a, ('xl', 'xh'), [(at(x), at((x + by) % 4)) for x in range(4)])  9.82 us
    pallas_call x3, Pallas kernels, local_call(): pl.pallas_call(function, out_shape=out_shape, in_specs=[vmem] * len(args)...  4.21 us
  transfers between devices with their start and end apart: 14, of which 6 were waited for; matrix products, arithmetic and copies ran while one was open for 3% of the time, Pallas kernels for 22%

profile of v3, /device:TPU:0, one launch (start us, length us, event | category | flops | bytes accessed | tf_op | source)
XLA Modules:
  0.0 97.7 jit_solution(6066188355682557978)
XLA Ops:
  0.6 2.6 %shard_map.94 = (bf16[2,1056,128]{2,1,0:T(8,128)(2,1)}, bf16[16,128,256]{2,1,0:T(8,128)(2,1)}) custom-call(bf16[8,128,128]{2,1,0:T(8,128)(2,1)} %q_ref.1, bf16[8,128,128]{2,1,0:T(8,128)(2,1)} %do_ref.1, bf16[8,128,128]{2,1,0:T(8,128)(2,1)} %o_ref.1, f32[8,128]{1,0:T(8,128)} %log_ref.1, bf16[128,128]{1,0:T(8,128)(2,1)} %k_ref.1, bf16[128,128]{1,0:T(8,128)(2,1)} %v_ref.1), custom_call_target="tpu_custom_call" | custom-call | tf_op jit(solution)/shard_map/pallas_call | solution.py:250
  3.2 1.7 %collective-permute-start.2 = (bf16[2,1056,128]{2,1,0:T(8,128)(2,1)}, bf16[2,1056,128]{2,1,0:T(8,128)(2,1)}, u32[]{:S(2)}, u32[]{:S(2)}) collective-permute-start(bf16[2,1056,128]{2,1,0:T(8,128)(2,1)} %get-tuple-element.20.rest_1_), channel_id=1, source_target_pairs={{0,16},{16,1},{1,17},{17,0},{2,18},{18,3},{3,19},{19,2},{4,20},{20... | collective-permute-start | bytes 1622024 | tf_op jit(solution)/shard_map/ppermute | solution.py:294
  4.9 1.6 %collective-permute-start.3 = (bf16[2,1056,128]{2,1,0:T(8,128)(2,1)}, bf16[2,1056,128]{2,1,0:T(8,128)(2,1)}, u32[]{:S(2)}, u32[]{:S(2)}) collective-permute-start(bf16[2,1056,128]{2,1,0:T(8,128)(2,1)} %get-tuple-element.20.rest_1_), channel_id=1, source_target_pairs={{0,17},{16,0},{1,16},{17,1},{2,19},{18,2},{3,18},{19,3},{4,21},{20... | collective-permute-start | bytes 1622024 | tf_op jit(solution)/shard_map/ppermute | solution.py:294
  6.5 1.9 %collective-permute-start.4 = (bf16[2,1056,128]{2,1,0:T(8,128)(2,1)}, bf16[2,1056,128]{2,1,0:T(8,128)(2,1)}, u32[]{:S(2)}, u32[]{:S(2)}) collective-permute-start(bf16[2,1056,128]{2,1,0:T(8,128)(2,1)} %get-tuple-element.20.rest_1_), channel_id=1, source_target_pairs={{0,1},{16,17},{1,0},{17,16},{2,3},{18,19},{3,2},{19,18},{4,5},{20,... | collective-permute-start | bytes 1622024 | tf_op jit(solution)/shard_map/ppermute | solution.py:294
  8.5 8.0 %all-to-all-start = ((bf16[16,128,256]{2,1,0:T(8,128)(2,1)}), bf16[16,128,256]{2,1,0:T(8,128)(2,1)S(1)}, u32[]{:S(2)}, u32[]{:S(2)}) async-start(bf16[16,128,256]{2,1,0:T(8,128)(2,1)} %get-tuple-element.19), calls=%async_computation | async-start | bytes 2097152 | tf_op jit(solution)/shard_map/all_to_all | solution.py:302
  17.5 0.2 convert_reduce_fusion.1
  17.8 1.6 %collective-permute-done.2.rest_5_ = bf16[2,1056,128]{2,1,0:T(8,128)(2,1)} collective-permute-done((bf16[2,1056,128]{2,1,0:T(8,128)(2,1)}, bf16[2,1056,128]{2,1,0:T(8,128)(2,1)}, u32[]{:S(2)}, u32[]{:S(2)}) %collective-permute-start.2) | collective-permute-done | bytes 540704 | tf_op jit(solution)/shard_map/ppermute | solution.py:294
  19.5 0.9 collective-permute-done.3.rest_6_
  20.4 11.8 %collective-permute-done.4.rest_7_ = bf16[2,1056,128]{2,1,0:T(8,128)(2,1)} collective-permute-done((bf16[2,1056,128]{2,1,0:T(8,128)(2,1)}, bf16[2,1056,128]{2,1,0:T(8,128)(2,1)}, u32[]{:S(2)}, u32[]{:S(2)}) %collective-permute-start.4) | collective-permute-done | bytes 540704 | tf_op jit(solution)/shard_map/ppermute | solution.py:294
  32.1 0.6 all-to-all-done
  32.7 8.6 %shard_map.95 = (f32[2,512,128]{2,1,0:T(8,128)S(1)}, bf16[2,512,128]{2,1,0:T(8,128)(2,1)S(1)}, bf16[2048,128]{1,0:T(8,128)(2,1)S(1)}, bf16[2048,128]{1,0:T(8,128...) custom-call(s32[32]{0:T(128)S(1)} %get-tuple-element.38.order, ...), custom_call_target="tpu_custom_call" | custom-call | flops 5368709120 | bytes 8388608 | tf_op jit(solution)/shard_map/pallas_call | solution.py:189
  41.3 0.7 copy-done.2
  42.0 12.4 %shard_map.96 = (f32[6,512,128]{2,1,0:T(8,128)S(1)}, f32[2048,128]{1,0:T(8,128)S(1)}, f32[2048,128]{1,0:T(8,128)S(1)}) custom-call(s32[32]{0:T(128)S(1)} %get-tuple-element.38.order, s32[32]{0:T(128)S(1)} %get-tuple-element.37.sorted_pos, s32[6]{0:T(128)S(1)} %get-tuple-element.47.query_block, s32[6]{0:T(128)S(1)} %get-tuple-element.48.below, ...), custom_call_target="tpu_custom_call" | custom-call | flops 8053063680 | bytes 8388608 | tf_op jit(solution)/shard_map/pallas_call | solution.py:189
  54.4 13.9 %shard_map.97 = (bf16[6,512,128]{2,1,0:T(8,128)(2,1)}, bf16[32,64,256]{2,1,0:T(8,128)(2,1)S(1)}) custom-call(s32[32]{0:T(128)S(1)} %get-tuple-element.38.order, s32[32]{0:T(128)S(1)} %get-tuple-element.37.sorted_pos, s32[6]{0:T(128)S(1)} %get-tuple-element.46.query_block, s32[6]{0:T(128)S(1)} %get-tuple-element.49.below, s32[6]{0:T(128)S(1)} %get-tuple-element.42.own, ...), custom_call_target="tpu_custom_call" | custom-call | flops 8053063680 | bytes 8388608 | tf_op jit(solution)/shard_map/pallas_call | solution.py:189
  68.4 1.0 copy-done
  69.4 7.7 %all-to-all-start.1 = ((bf16[16,128,256]{2,1,0:T(8,128)(2,1)}), bf16[16,128,256]{2,1,0:T(8,128)(2,1)S(1)}, u32[]{:S(2)}, u32[]{:S(2)}) async-start(bf16[16,128,256]{2,1,0:T(8,128)(2,1)} %bitcast.14), calls=%async_computation.1 | async-start | bytes 2097152 | tf_op jit(solution)/shard_map/all_to_all | solution.py:302
  77.0 0.3 collective-permute-start.1
  77.3 1.3 %add_convert_fusion = bf16[6,512,128]{2,1,0:T(8,128)(2,1)S(1)} fusion(f32[6,512,128]{2,1,0:T(8,128)S(1)} %get-tuple-element.28, bf16[6,512,128]{2,1,0:T(8,128)(2,1)} %collective-permute-done.8), kind=kLoop, calls=%fused_computation | loop fusion | flops 1179648 | bytes 3145728 | tf_op jit(solution)/shard_map/convert_element_type | solution.py:354
  78.7 3.0 %collective-permute-start.9 = (bf16[2,512,128]{2,1,0:T(8,128)(2,1)S(1)}, bf16[2,512,128]{2,1,0:T(8,128)(2,1)S(1)}, u32[]{:S(2)}, u32[]{:S(2)}) collective-permute-start(bf16[2,512,128]{2,1,0:T(8,128)(2,1)S(1)} %get-tuple-element.41), channel_id=1, source_target_pairs={{0,17},{16,0},{1,16},{17,1},{2,19},{18,2},{3,18},{19,3},{4,21},{20... | collective-permute-start | bytes 786440 | tf_op jit(solution)/shard_map/ppermute | solution.py:294
  81.7 1.5 %collective-permute-start.11 = (bf16[2,512,128]{2,1,0:T(8,128)(2,1)S(1)}, bf16[2,512,128]{2,1,0:T(8,128)(2,1)S(1)}, u32[]{:S(2)}, u32[]{:S(2)}) collective-permute-start(bf16[2,512,128]{2,1,0:T(8,128)(2,1)S(1)} %get-tuple-element.39), channel_id=1, source_target_pairs={{0,1},{16,17},{1,0},{17,16},{2,3},{18,19},{3,2},{19,18},{4,5},{20,... | collective-permute-start | bytes 786440 | tf_op jit(solution)/shard_map/ppermute | solution.py:294
  83.3 10.6 %all-to-all-done.1.parts_ref = bf16[16,128,256]{2,1,0:T(8,128)(2,1)S(1)} async-done(((bf16[16,128,256]{2,1,0:T(8,128)(2,1)}), bf16[16,128,256]{2,1,0:T(8,128)(2,1)S(1)}, u32[]{:S(2)}, u32[]{:S(2)}) %all-to-all-start.1) | async-done | bytes 1048608 | tf_op jit(solution)/shard_map/all_to_all | solution.py:302
  93.9 0.8 shard_map.99
  94.6 2.2 %collective-permute-done.10.rest_2_ = bf16[2,512,128]{2,1,0:T(8,128)(2,1)S(1)} collective-permute-done((bf16[2,512,128]{2,1,0:T(8,128)(2,1)S(1)}, bf16[2,512,128]{2,1,0:T(8,128)(2,1)S(1)}, u32[]{:S(2)}, u32[]{:S(2)}) %collective-permute-start.10) | collective-permute-done | bytes 262176 | tf_op jit(solution)/shard_map/ppermute | solution.py:294
  96.8 0.9 shard_map.98
  (33 shorter events, 1.1 us)
Async XLA Ops:
  0.6 16.3 %copy-start.3 = (s32[256]{0:T(256)S(1)}, s32[256]{0:T(256)}, u32[]{:S(2)}) copy-start(s32[256]{0:T(256)} %param.13) | copy-start | bytes 3076
  3.2 29.5 %copy-start.1 = (bf16[2,1056,128]{2,1,0:T(8,128)(2,1)S(1)}, bf16[2,1056,128]{2,1,0:T(8,128)(2,1)}, u32[]{:S(2)}) copy-start(bf16[2,1056,128]{2,1,0:T(8,128)(2,1)} %get-tuple-element.20.rest_1_) | copy-start | bytes 1622020
  3.2 28.9 %collective-permute-start = (bf16[2,1056,128]{2,1,0:T(8,128)(2,1)}, bf16[2,1056,128]{2,1,0:T(8,128)(2,1)S(1)}, u32[]{:S(2)}, u32[]{:S(2)}) collective-permute-start(bf16[2,1056,128]{2,1,0:T(8,128)(2,1)} %get-tuple-element.20.rest_1_), channel_id=1, source_target_pairs={{0,8},{8,0},{1,9},{9,1},{2,10},{10,2},{3,11},{11,3},{4,12},{12,4},... | collective-permute-start | bytes 1622024 | tf_op jit(solution)/shard_map/ppermute | solution.py:298
  3.2 16.2 %collective-permute-start.2 = (bf16[2,1056,128]{2,1,0:T(8,128)(2,1)}, bf16[2,1056,128]{2,1,0:T(8,128)(2,1)}, u32[]{:S(2)}, u32[]{:S(2)}) collective-permute-start(bf16[2,1056,128]{2,1,0:T(8,128)(2,1)} %get-tuple-element.20.rest_1_), channel_id=1, source_target_pairs={{0,16},{16,1},{1,17},{17,0},{2,18},{18,3},{3,19},{19,2},{4,20},{20... | collective-permute-start | bytes 1622024 | tf_op jit(solution)/shard_map/ppermute | solution.py:294
  4.9 15.5 %collective-permute-start.3 = (bf16[2,1056,128]{2,1,0:T(8,128)(2,1)}, bf16[2,1056,128]{2,1,0:T(8,128)(2,1)}, u32[]{:S(2)}, u32[]{:S(2)}) collective-permute-start(bf16[2,1056,128]{2,1,0:T(8,128)(2,1)} %get-tuple-element.20.rest_1_), channel_id=1, source_target_pairs={{0,17},{16,0},{1,16},{17,1},{2,19},{18,2},{3,18},{19,3},{4,21},{20... | collective-permute-start | bytes 1622024 | tf_op jit(solution)/shard_map/ppermute | solution.py:294
  6.5 25.6 %collective-permute-start.4 = (bf16[2,1056,128]{2,1,0:T(8,128)(2,1)}, bf16[2,1056,128]{2,1,0:T(8,128)(2,1)}, u32[]{:S(2)}, u32[]{:S(2)}) collective-permute-start(bf16[2,1056,128]{2,1,0:T(8,128)(2,1)} %get-tuple-element.20.rest_1_), channel_id=1, source_target_pairs={{0,1},{16,17},{1,0},{17,16},{2,3},{18,19},{3,2},{19,18},{4,5},{20,... | collective-permute-start | bytes 1622024 | tf_op jit(solution)/shard_map/ppermute | solution.py:294
  8.5 24.2 %all-to-all-start = ((bf16[16,128,256]{2,1,0:T(8,128)(2,1)}), bf16[16,128,256]{2,1,0:T(8,128)(2,1)S(1)}, u32[]{:S(2)}, u32[]{:S(2)}) async-start(bf16[16,128,256]{2,1,0:T(8,128)(2,1)} %get-tuple-element.19), calls=%async_computation | async-start | bytes 2097152 | tf_op jit(solution)/shard_map/all_to_all | solution.py:302
  19.4 35.0 %collective-permute-start.5 = (bf16[2,1056,128]{2,1,0:T(8,128)(2,1)}, bf16[2,1056,128]{2,1,0:T(8,128)(2,1)}, u32[]{:S(2)}, u32[]{:S(2)}) collective-permute-start(bf16[2,1056,128]{2,1,0:T(8,128)(2,1)} %collective-permute-done.2.rest_5_), channel_id=1, source_target_pairs={{0,8},{8,0},{1,9},{9,1},{2,10},{10,2},{3,11},{11,3},{4,12},{12,4},... | collective-permute-start | bytes 1622024 | tf_op jit(solution)/shard_map/ppermute | solution.py:298
  20.4 34.1 %collective-permute-start.6 = (bf16[2,1056,128]{2,1,0:T(8,128)(2,1)}, bf16[2,1056,128]{2,1,0:T(8,128)(2,1)}, u32[]{:S(2)}, u32[]{:S(2)}) collective-permute-start(bf16[2,1056,128]{2,1,0:T(8,128)(2,1)} %collective-permute-done.3.rest_6_), channel_id=1, source_target_pairs={{0,8},{8,0},{1,9},{9,1},{2,10},{10,2},{3,11},{11,3},{4,12},{12,4},... | collective-permute-start | bytes 1622024 | tf_op jit(solution)/shard_map/ppermute | solution.py:298
  32.1 22.3 %collective-permute-start.7 = (bf16[2,1056,128]{2,1,0:T(8,128)(2,1)}, bf16[2,1056,128]{2,1,0:T(8,128)(2,1)}, u32[]{:S(2)}, u32[]{:S(2)}) collective-permute-start(bf16[2,1056,128]{2,1,0:T(8,128)(2,1)} %collective-permute-done.4.rest_7_), channel_id=1, source_target_pairs={{0,8},{8,0},{1,9},{9,1},{2,10},{10,2},{3,11},{11,3},{4,12},{12,4},... | collective-permute-start | bytes 1622024 | tf_op jit(solution)/shard_map/ppermute | solution.py:298
  41.3 0.7 copy-start.2
  68.4 1.0 copy-start
  69.3 8.0 %collective-permute-start.8 = (bf16[6,512,128]{2,1,0:T(8,128)(2,1)}, bf16[6,512,128]{2,1,0:T(8,128)(2,1)}, u32[]{:S(2)}, u32[]{:S(2)}) collective-permute-start(bf16[6,512,128]{2,1,0:T(8,128)(2,1)} %get-tuple-element.31), channel_id=1, source_target_pairs={{0,8},{8,0},{1,9},{9,1},{2,10},{10,2},{3,11},{11,3},{4,12},{12,4},... | collective-permute-start | bytes 2359304 | tf_op jit(solution)/shard_map/ppermute | solution.py:298
  69.4 24.5 %all-to-all-start.1 = ((bf16[16,128,256]{2,1,0:T(8,128)(2,1)}), bf16[16,128,256]{2,1,0:T(8,128)(2,1)S(1)}, u32[]{:S(2)}, u32[]{:S(2)}) async-start(bf16[16,128,256]{2,1,0:T(8,128)(2,1)} %bitcast.14), calls=%async_computation.1 | async-start | bytes 2097152 | tf_op jit(solution)/shard_map/all_to_all | solution.py:302
  77.0 17.6 %collective-permute-start.1 = (bf16[2,512,128]{2,1,0:T(8,128)(2,1)}, bf16[2,512,128]{2,1,0:T(8,128)(2,1)S(1)}, u32[]{:S(2)}, u32[]{:S(2)}) collective-permute-start(bf16[2,512,128]{2,1,0:T(8,128)(2,1)} %copy-done.2), channel_id=1, source_target_pairs={{0,8},{8,0},{1,9},{9,1},{2,10},{10,2},{3,11},{11,3},{4,12},{12,4},... | collective-permute-start | bytes 786440 | tf_op jit(solution)/shard_map/ppermute | solution.py:298
  78.7 15.9 %collective-permute-start.9 = (bf16[2,512,128]{2,1,0:T(8,128)(2,1)S(1)}, bf16[2,512,128]{2,1,0:T(8,128)(2,1)S(1)}, u32[]{:S(2)}, u32[]{:S(2)}) collective-permute-start(bf16[2,512,128]{2,1,0:T(8,128)(2,1)S(1)} %get-tuple-element.41), channel_id=1, source_target_pairs={{0,17},{16,0},{1,16},{17,1},{2,19},{18,2},{3,18},{19,3},{4,21},{20... | collective-permute-start | bytes 786440 | tf_op jit(solution)/shard_map/ppermute | solution.py:294
  81.7 15.0 %collective-permute-start.10 = (bf16[2,512,128]{2,1,0:T(8,128)(2,1)S(1)}, bf16[2,512,128]{2,1,0:T(8,128)(2,1)S(1)}, u32[]{:S(2)}, u32[]{:S(2)}) collective-permute-start(bf16[2,512,128]{2,1,0:T(8,128)(2,1)S(1)} %get-tuple-element.40), channel_id=1, source_target_pairs={{0,16},{16,1},{1,17},{17,0},{2,18},{18,3},{3,19},{19,2},{4,20},{20... | collective-permute-start | bytes 786440 | tf_op jit(solution)/shard_map/ppermute | solution.py:294
  81.7 15.0 %collective-permute-start.11 = (bf16[2,512,128]{2,1,0:T(8,128)(2,1)S(1)}, bf16[2,512,128]{2,1,0:T(8,128)(2,1)S(1)}, u32[]{:S(2)}, u32[]{:S(2)}) collective-permute-start(bf16[2,512,128]{2,1,0:T(8,128)(2,1)S(1)} %get-tuple-element.39), channel_id=1, source_target_pairs={{0,1},{16,17},{1,0},{17,16},{2,3},{18,19},{3,2},{19,18},{4,5},{20,... | collective-permute-start | bytes 786440 | tf_op jit(solution)/shard_map/ppermute | solution.py:294
